TPU v7x, 32 devices: a whole 2x2x4 slice. The times are simulated.
32 devices in a mesh: seq: 8 (over z, x), fsdp: 4 (over y, core).
Axes of the slice: x: 2, y: 2, z: 4, core: 2. Of those that a mesh axis runs over, the one named last changes fastest.
Arguments:
- layer_input: bfloat16 [4, 1024, 1024], P('fsdp', 'seq'), may hold values from -6 to 6
- doc_lengths: int32 [4, 5], replicated, may hold values from 1 to 512, 1024 in all within a row
- attn_gain: bfloat16 [1024], P(('seq', 'fsdp')), may hold values from 0.5 to 1.5
- qkv_weight: bfloat16 [1024, 3, 1024], P('seq', None, 'fsdp'), may hold values from -2 to 2
- out_weight: bfloat16 [1024, 1024], P('fsdp', 'seq'), may hold values from -0.5 to 0.5
- mlp_gain: bfloat16 [1024], P(('seq', 'fsdp')), may hold values from 0.5 to 1.5
- in_weight: bfloat16 [1024, 2, 2624], P('seq', None, 'fsdp'), may hold values from -0.1875 to 0.1875
- down_weight: bfloat16 [1024, 2624], P('seq', 'fsdp'), may hold values from -0.125 to 0.125
- out_grad: bfloat16 [4, 1024, 1024], P('fsdp', 'seq'), may hold values from -6 to 6
Outputs:
- layer_output: bfloat16 [4, 1024, 1024], P('fsdp', 'seq')
- input_grad: float32 [4, 1024, 1024], P('fsdp', 'seq')
- attn_gain_grad: float32 [1024], P(('seq', 'fsdp'))
- qkv_weight_grad: float32 [1024, 3, 1024], P('seq', None, 'fsdp')
- out_weight_grad: float32 [1024, 1024], P('fsdp', 'seq')
- mlp_gain_grad: float32 [1024], P(('seq', 'fsdp'))
- in_weight_grad: float32 [1024, 2, 2624], P('seq', None, 'fsdp')
- down_weight_grad: float32 [1024, 2624], P('seq', 'fsdp')
Inputs may be any that keep to these rules, and one draw needn't show every extreme that they name: Each row of doc_lengths lists the lengths of the documents of one stream in order; they sum to 1024 and the longest is exactly 512.
All inputs are finite; a program needn't handle non-finite values.
Results may differ from a plain program's by a relative error of at most 0.02.
Values may be sent and summed in bfloat16 or wider, within the bound.
A program may use at most 128 MiB of HBM per device.

v0:
```python
import jax
import jax.numpy as jnp
from jax import lax
from jax.sharding import PartitionSpec as P

HEAD = 64
WIN = 64


EPSILON = 1e-05


def with_halo(value, sides, width):
    for axis, dim in sides:
        devices, length = (lax.axis_size(axis), value.shape[dim])
        up = [(i, (i + 1) % devices) for i in range(devices - 1)]
        down = [(j, i) for i, j in up]
        last = lax.slice_in_dim(value, length - width, length, axis=dim)
        first = lax.slice_in_dim(value, 0, width, axis=dim)
        before = lax.ppermute(last, axis, up)
        after = lax.ppermute(first, axis, down)
        value = jnp.concatenate([before, value, after], axis=dim)
    return value


def norm_forward(values, gain):
    mean = jnp.mean(values, axis=-1, keepdims=True)
    centred = values - mean
    inverse = lax.rsqrt(jnp.mean(centred * centred, axis=-1, keepdims=True) + EPSILON)
    scaled = centred * inverse
    return (scaled, inverse, (scaled * gain.astype(jnp.float32)).astype(jnp.bfloat16))


def norm_backward(grad, scaled, inverse, gain):
    weighted = grad * gain.astype(jnp.float32)
    back = inverse * (
        weighted
        - jnp.mean(weighted, axis=-1, keepdims=True)
        - scaled * jnp.mean(weighted * scaled, axis=-1, keepdims=True)
    )
    return (back, jnp.sum(grad * scaled, axis=0))


def gelu_parts(inner):
    cdf = 0.5 * (1.0 + jax.scipy.special.erf(inner * 0.7071067811865476))
    density = jnp.exp(-0.5 * inner * inner) * 0.3989422804014327
    return (inner * cdf, cdf + inner * density)


def rope_tables(positions, head_size):
    half = head_size // 2
    inv_freq = 10000.0 ** (-(2.0 / head_size) * jnp.arange(half, dtype=jnp.float32))
    angle = positions.astype(jnp.float32)[:, None] * inv_freq[None, :]
    return (jnp.cos(angle)[:, None, :], jnp.sin(angle)[:, None, :])


def rotate(field, cosine, sine):
    half = field.shape[-1] // 2
    first, second = (field[..., :half], field[..., half:])
    return jnp.concatenate(
        [first * cosine - second * sine, second * cosine + first * sine], axis=-1
    )


def unrotate(grad, cosine, sine):
    half = grad.shape[-1] // 2
    first, second = (grad[..., :half], grad[..., half:])
    return jnp.concatenate(
        [first * cosine + second * sine, second * cosine - first * sine], axis=-1
    )


def doc_ids(lengths_row, positions):
    starts = jnp.cumsum(lengths_row, dtype=jnp.int32) - lengths_row
    total = jnp.sum(lengths_row, dtype=jnp.int32)
    found = (
        jnp.sum((positions[:, None] >= starts[None, :]).astype(jnp.int32), axis=1, dtype=jnp.int32)
        - 1
    )
    valid = (positions >= 0) & (positions < total)
    return jnp.where(valid, found, -1)


def window_mask(ids_query, ids_key, reach):
    block = ids_query.shape[0]
    offset = (
        jnp.arange(block, dtype=jnp.int32)[:, None]
        + reach
        - jnp.arange(block + 2 * reach, dtype=jnp.int32)[None, :]
    )
    return (jnp.abs(offset) <= reach) & (ids_query[:, None] == ids_key[None, :])


def attend_forward(query, keys, values, allowed):
    scale = query.shape[-1] ** (-0.5)
    scores = jnp.einsum("nhe,mhe->hnm", query, keys, preferred_element_type=jnp.float32) * scale
    masked = jnp.where(allowed[None], scores, -1e30)
    top = jnp.max(masked, axis=-1, keepdims=True)
    expd = jnp.exp(masked - top)
    total = jnp.sum(expd, axis=-1, keepdims=True)
    log_total = (top + jnp.log(total))[..., 0]
    probs = (expd / total).astype(jnp.bfloat16)
    out = jnp.einsum("hnm,mhe->nhe", probs, values, preferred_element_type=jnp.float32)
    return (out.astype(jnp.bfloat16), log_total)


def attend_backward(query, keys, values, allowed, log_total, attended, grad_out):
    scale = query.shape[-1] ** (-0.5)
    scores = jnp.einsum("nhe,mhe->hnm", query, keys, preferred_element_type=jnp.float32) * scale
    masked = jnp.where(allowed[None], scores, -1e30)
    again = jnp.exp(masked - log_total[..., None])
    again_b = again.astype(jnp.bfloat16)
    grad_values = jnp.einsum("hnm,nhe->mhe", again_b, grad_out, preferred_element_type=jnp.float32)
    grad_probs = jnp.einsum("nhe,mhe->hnm", grad_out, values, preferred_element_type=jnp.float32)
    delta = jnp.sum(grad_out.astype(jnp.float32) * attended.astype(jnp.float32), axis=-1).T
    grad_scores = (again * (grad_probs - delta[..., None]) * scale).astype(jnp.bfloat16)
    grad_query = jnp.einsum("hnm,mhe->nhe", grad_scores, keys, preferred_element_type=jnp.float32)
    grad_keys = jnp.einsum("hnm,nhe->mhe", grad_scores, query, preferred_element_type=jnp.float32)
    return (grad_query, grad_keys, grad_values)


def attention_forward(query, ext_keys, ext_values, ids_query, ids_key, block, reach):
    rows, heads = (query.shape[0], query.shape[1])
    count = rows // block

    def step(carry, index):
        allowed = window_mask(ids_query, ids_key, reach)
        return (carry, attend_forward(query, ext_keys, ext_values, allowed))

    _, (outs, totals) = lax.scan(
        step, jnp.zeros((), jnp.float32), jnp.arange(count, dtype=jnp.int32)
    )
    return (outs.reshape(rows, heads, -1), totals.transpose(1, 0, 2).reshape(heads, rows))


def attention_backward(
    query, ext_keys, ext_values, ids_query, ids_key, log_total, attended, grad_out, block, reach
):
    rows = query.shape[0]
    count = rows // block
    zero = jnp.zeros(ext_keys.shape, jnp.float32)

    def step(carry, index):
        keys_acc, values_acc = carry
        allowed = window_mask(ids_query, ids_key, reach)
        grad_query, grad_keys, grad_values = attend_backward(
            query, ext_keys, ext_values, allowed, log_total, attended, grad_out
        )
        keys_acc = keys_acc + grad_keys
        values_acc = values_acc + grad_values
        return ((keys_acc, values_acc), grad_query)

    (keys_acc, values_acc), grads = lax.scan(step, (zero, zero), jnp.arange(count, dtype=jnp.int32))
    return (grads.reshape(query.shape), keys_acc, values_acc)


def per_device(
    layer_input,
    doc_lengths,
    attn_gain,
    qkv_weight,
    out_weight,
    mlp_gain,
    in_weight,
    down_weight,
    out_grad,
):
    tokens = layer_input[0]
    grad_rows = out_grad[0]
    rows = tokens.shape[0]
    width = tokens.shape[1]
    streams = doc_lengths.shape[0]
    quarter = qkv_weight.shape[2]
    heads_here = quarter // HEAD
    share = down_weight.shape[1]
    reach = WIN
    block = min(rows, 512)
    first = lax.axis_index("seq") * rows
    positions = first + jnp.arange(rows, dtype=jnp.int32)
    outer = first - reach + jnp.arange(rows + 2 * reach, dtype=jnp.int32)
    ids_query = jax.vmap(doc_ids, in_axes=(0, None))(doc_lengths, positions)
    ids_key = jax.vmap(doc_ids, in_axes=(0, None))(doc_lengths, outer)
    cosine, sine = rope_tables(positions, HEAD)
    gain_one, gain_two = (
        lax.all_gather(attn_gain, ("seq", "fsdp"), axis=0, tiled=True),
        lax.all_gather(mlp_gain, ("seq", "fsdp"), axis=0, tiled=True),
    )
    qkv_full, out_rows, in_full, down_full = (
        lax.all_gather(qkv_weight, "seq", axis=0, tiled=True),
        lax.all_gather(out_weight, "seq", axis=1, tiled=True),
        lax.all_gather(in_weight, "seq", axis=0, tiled=True),
        lax.all_gather(down_weight, "seq", axis=0, tiled=True),
    )
    qkv_flat = qkv_full.reshape(width, 3 * quarter)
    in_flat = in_full.reshape(width, 2 * share)
    resid_in = tokens.astype(jnp.float32)
    scaled_one, inverse_one, normed_one = norm_forward(resid_in, gain_one)
    normed_group = lax.all_gather(normed_one[None], "fsdp", axis=0, tiled=True)
    group_one = normed_group.reshape(streams * rows, width)
    projected = jnp.dot(group_one, qkv_flat, preferred_element_type=jnp.float32)
    split = projected.reshape(streams, rows, 3, heads_here, HEAD)
    query = rotate(split[:, :, 0], cosine, sine).astype(jnp.bfloat16)
    keys = rotate(split[:, :, 1], cosine, sine).astype(jnp.bfloat16)
    values = split[:, :, 2].astype(jnp.bfloat16)
    packed = jnp.concatenate(
        [keys.reshape(streams, rows, quarter), values.reshape(streams, rows, quarter)], axis=2
    )
    extended = with_halo(packed, (("seq", 1),), WIN)
    ext_keys = extended[:, :, :quarter].reshape(streams, -1, heads_here, HEAD)
    ext_values = extended[:, :, quarter:].reshape(streams, -1, heads_here, HEAD)

    def forward_stream(stream_query, stream_keys, stream_values, stream_ids, stream_key_ids):
        return attention_forward(
            stream_query, stream_keys, stream_values, stream_ids, stream_key_ids, block, reach
        )

    attended, log_total = jax.vmap(forward_stream)(query, ext_keys, ext_values, ids_query, ids_key)
    attended_flat = attended.reshape(streams * rows, quarter)
    partial_attn = jnp.dot(attended_flat, out_rows, preferred_element_type=jnp.float32)
    attn_sum = lax.psum_scatter(
        partial_attn.reshape(streams, rows, width).astype(jnp.bfloat16),
        "fsdp",
        scatter_dimension=0,
        tiled=True,
    ).astype(jnp.float32)
    middle = resid_in + attn_sum[0]
    scaled_two, inverse_two, normed_two = norm_forward(middle, gain_two)
    normed_all, grad_all = (
        lax.all_gather(normed_two[None], "fsdp", axis=0, tiled=True),
        lax.all_gather(grad_rows[None], "fsdp", axis=0, tiled=True),
    )
    normed_flat = normed_all.reshape(streams * rows, width)
    grad_flat = grad_all.reshape(streams * rows, width)
    hidden = jnp.dot(normed_flat, in_flat, preferred_element_type=jnp.float32)
    inner, gate = (hidden[:, :share], hidden[:, share:])
    activated, slope = gelu_parts(inner)
    mixed = (activated * gate).astype(jnp.bfloat16)
    partial_down = lax.dot_general(
        mixed, down_full, (((1,), (1,)), ((), ())), preferred_element_type=jnp.float32
    )
    projected_down = lax.psum_scatter(
        partial_down.reshape(streams, rows, width).astype(jnp.bfloat16),
        "fsdp",
        scatter_dimension=0,
        tiled=True,
    ).astype(jnp.float32)
    output = (middle + projected_down[0]).astype(jnp.bfloat16)
    qkv_full, out_rows, in_full, down_full = (
        lax.all_gather(qkv_weight, "seq", axis=0, tiled=True),
        lax.all_gather(out_weight, "seq", axis=1, tiled=True),
        lax.all_gather(in_weight, "seq", axis=0, tiled=True),
        lax.all_gather(down_weight, "seq", axis=0, tiled=True),
    )
    qkv_flat = qkv_full.reshape(width, 3 * quarter)
    in_flat = in_full.reshape(width, 2 * share)
    grad_down = lax.dot_general(
        grad_flat, mixed, (((0,), (0,)), ((), ())), preferred_element_type=jnp.float32
    )
    grad_mixed = jnp.dot(grad_flat, down_full, preferred_element_type=jnp.float32)
    grad_hidden = jnp.concatenate(
        [grad_mixed * gate * slope, grad_mixed * activated], axis=1
    ).astype(jnp.bfloat16)
    grad_in = lax.dot_general(
        normed_flat, grad_hidden, (((0,), (0,)), ((), ())), preferred_element_type=jnp.float32
    )
    partial_back = lax.dot_general(
        grad_hidden, in_flat, (((1,), (1,)), ((), ())), preferred_element_type=jnp.float32
    )
    grad_normed_two = lax.psum_scatter(
        partial_back.reshape(streams, rows, width).astype(jnp.bfloat16),
        "fsdp",
        scatter_dimension=0,
        tiled=True,
    ).astype(jnp.float32)[0]
    back_two, grad_gain_two = norm_backward(grad_normed_two, scaled_two, inverse_two, gain_two)
    grad_middle = grad_rows.astype(jnp.float32) + back_two
    grad_middle_b = grad_middle.astype(jnp.bfloat16)
    grad_group = lax.all_gather(grad_middle_b[None], "fsdp", axis=0, tiled=True).reshape(
        streams * rows, width
    )
    grad_out_weight = lax.dot_general(
        attended_flat, grad_group, (((0,), (0,)), ((), ())), preferred_element_type=jnp.float32
    )
    grad_attended = lax.dot_general(
        grad_group, out_rows, (((1,), (1,)), ((), ())), preferred_element_type=jnp.float32
    ).astype(jnp.bfloat16)

    def backward_stream(
        stream_query,
        stream_keys,
        stream_values,
        stream_ids,
        stream_key_ids,
        stream_total,
        stream_attended,
        stream_grad,
    ):
        return attention_backward(
            stream_query,
            stream_keys,
            stream_values,
            stream_ids,
            stream_key_ids,
            stream_total,
            stream_attended,
            stream_grad,
            block,
            reach,
        )

    grad_query, keys_acc, values_acc = jax.vmap(backward_stream)(
        query,
        ext_keys,
        ext_values,
        ids_query,
        ids_key,
        log_total,
        attended,
        grad_attended.reshape(streams, rows, heads_here, HEAD),
    )
    rims = jnp.concatenate(
        [keys_acc.reshape(streams, -1, quarter), values_acc.reshape(streams, -1, quarter)], axis=2
    )
    edges = jnp.concatenate([rims[:, :reach], rims[:, -reach:]], axis=1)
    arrived = with_halo(edges.astype(jnp.bfloat16), (("seq", 1),), WIN).astype(edges.dtype)
    owned = (
        rims[:, reach : reach + rows]
        + jnp.pad(arrived[:, :reach], ((0, 0), (0, rows - reach), (0, 0)))
        + jnp.pad(arrived[:, -reach:], ((0, 0), (rows - reach, 0), (0, 0)))
    )
    grad_keys = unrotate(
        owned[:, :, :quarter].reshape(streams, rows, heads_here, HEAD), cosine, sine
    )
    grad_values = owned[:, :, quarter:]
    grad_query = unrotate(grad_query, cosine, sine)
    grad_projected = jnp.concatenate(
        [
            grad_query.reshape(streams * rows, quarter),
            grad_keys.reshape(streams * rows, quarter),
            grad_values.reshape(streams * rows, quarter),
        ],
        axis=1,
    ).astype(jnp.bfloat16)
    grad_qkv = lax.dot_general(
        group_one, grad_projected, (((0,), (0,)), ((), ())), preferred_element_type=jnp.float32
    )
    partial_one = lax.dot_general(
        grad_projected, qkv_flat, (((1,), (1,)), ((), ())), preferred_element_type=jnp.float32
    )
    grad_normed_one = lax.psum_scatter(
        partial_one.reshape(streams, rows, width).astype(jnp.bfloat16),
        "fsdp",
        scatter_dimension=0,
        tiled=True,
    ).astype(jnp.float32)[0]
    back_one, grad_gain_one = norm_backward(grad_normed_one, scaled_one, inverse_one, gain_one)
    input_grad = grad_middle + back_one
    summed_qkv, summed_out, summed_in, summed_down = (
        lax.psum_scatter(
            grad_qkv.reshape(width, 3, quarter), "seq", scatter_dimension=0, tiled=True
        ),
        lax.psum_scatter(grad_out_weight, "seq", scatter_dimension=1, tiled=True),
        lax.psum_scatter(grad_in.reshape(width, 2, share), "seq", scatter_dimension=0, tiled=True),
        lax.psum_scatter(grad_down, "seq", scatter_dimension=0, tiled=True),
    )
    summed_gain_one, summed_gain_two = (
        lax.psum_scatter(grad_gain_one, ("seq", "fsdp"), scatter_dimension=0, tiled=True),
        lax.psum_scatter(grad_gain_two, ("seq", "fsdp"), scatter_dimension=0, tiled=True),
    )
    return (
        output[None],
        input_grad[None],
        summed_gain_one,
        summed_qkv,
        summed_out,
        summed_gain_two,
        summed_in,
        summed_down,
    )


def solution(mesh):
    in_specs = (
        P("fsdp", "seq", None),
        P(),
        P(("seq", "fsdp")),
        P("seq", None, "fsdp"),
        P("fsdp", "seq"),
        P(("seq", "fsdp")),
        P("seq", None, "fsdp"),
        P("seq", "fsdp"),
        P("fsdp", "seq", None),
    )
    out_specs = (
        P("fsdp", "seq", None),
        P("fsdp", "seq", None),
        P(("seq", "fsdp")),
        P("seq", None, "fsdp"),
        P("fsdp", "seq"),
        P(("seq", "fsdp")),
        P("seq", None, "fsdp"),
        P("seq", "fsdp"),
    )
    return jax.shard_map(
        per_device, mesh=mesh, in_specs=in_specs, out_specs=out_specs, check_vma=False
    )
```

profile of v0, /device:TPU:0, one launch (start us, length us, event | category | flops | bytes accessed | tf_op | source)
XLA Modules:
  0.0 815.5 jit_solution(5662635997442417773)
XLA Ops:
  8.9 42.0 %all-reduce.6 = (bf16[1024]{0:T(1024)(128)(2,1)S(1)}, bf16[1024]{0:T(1024)(128)(2,1)S(1)}) all-reduce(bf16[1024]{0:T(1024)(128)(2,1)S(1)} %dynamic-update-slice, bf16[1024]{0:T(1024)(128)(2,1)S(1)} %dynamic-update-slice.1), channel_id=1, replica_groups=mesh['seq'=8,'fsdp'=4] {'seq','fsdp'}, use_global_device_ids=true, to_apply=%add.1 | all-reduce | flops 2048 | bytes 8192
  59.4 12.4 %all-gather.8.cloned.1.call-done = bf16[4,128,1024]{2,1,0:T(8,128)(2,1)} async-done(((bf16[1,128,1024]{2,1,0:T(8,128)(2,1)}), bf16[4,128,1024]{2,1,0:T(8,128)(2,1)}) %all-gather.8.cloned.1.call-update) | async-done | bytes 1048592 | tf_op jit(solution)/shard_map/all_gather | solution.py:198
  71.7 47.1 %all-gather.10.cloned.1.call-done = bf16[1024,3,256]{0,2,1:T(8,128)(2,1)} async-done(((bf16[128,3,256]{0,2,1:T(8,128)(2,1)}), bf16[1024,3,256]{0,2,1:T(8,128)(2,1)}) %all-gather.10.cloned.1.call-update) | async-done | bytes 1572880 | tf_op jit(solution)/shard_map/all_gather | solution.py:189
  123.4 4.6 collective-permute-start
  128.2 42.3 %all_gather.37 = bf16[256,1024]{1,0:T(8,128)(2,1)S(1)} all-gather(bf16[256,128]{1,0:T(8,128)(2,1)S(1)} %copy-done.30), channel_id=1, replica_groups=mesh['seq'=8,'fsdp'=4] {'seq'}, dimensions={1}, use_global_device_ids=true | all-gather | bytes 589824 | tf_op jit(solution)/shard_map/all_gather | solution.py:190
  176.3 22.6 %reduce-scatter.9.cloned.1.call-done = bf16[1,128,1024]{2,1,0:T(8,128)(2,1)} async-done(((bf16[4,128,1024]{2,1,0:T(8,128)(2,1)}), bf16[1,128,1024]{2,1,0:T(8,128)(2,1)}) %reduce-scatter.9.cloned.1.call-update) | async-done | bytes 262160 | tf_op jit(solution)/shard_map/reduce_scatter | solution.py:220
  204.4 53.6 %all-gather.14.cloned.1.call-done = bf16[1024,2,656]{0,2,1:T(8,128)(2,1)} async-done(((bf16[128,2,656]{0,2,1:T(8,128)(2,1)}), bf16[1024,2,656]{0,2,1:T(8,128)(2,1)}) %all-gather.14.cloned.1.call-update) | async-done | bytes 2686992 | tf_op jit(solution)/shard_map/all_gather | solution.py:191
  258.1 16.9 %all-gather.12.cloned.1.call-done = bf16[4,128,1024]{2,1,0:T(8,128)(2,1)} async-done(((bf16[1,128,1024]{2,1,0:T(8,128)(2,1)}), bf16[4,128,1024]{2,1,0:T(8,128)(2,1)}) %all-gather.12.cloned.1.call-update) | async-done | bytes 1048592 | tf_op jit(solution)/shard_map/all_gather | solution.py:229
  275.0 5.2 fusion.71
  280.2 12.9 %all-gather.18.cloned.1.call-done = bf16[4,128,1024]{2,1,0:T(8,128)(2,1)} async-done(((bf16[1,128,1024]{2,1,0:T(8,128)(2,1)}), bf16[4,128,1024]{2,1,0:T(8,128)(2,1)}) %all-gather.18.cloned.1.call-update) | async-done | bytes 1048592 | tf_op jit(solution)/shard_map/all_gather | solution.py:230
  293.1 44.0 %all-gather.16.cloned.1.call-done = bf16[1024,656]{0,1:T(8,128)(2,1)} async-done(((bf16[128,656]{0,1:T(8,128)(2,1)}), bf16[1024,656]{0,1:T(8,128)(2,1)}) %all-gather.16.cloned.1.call-update) | async-done | bytes 1343504 | tf_op jit(solution)/shard_map/all_gather | solution.py:192
  337.1 4.7 fusion.8
  347.1 22.9 %reduce-scatter.13.cloned.1.call-done = bf16[1,128,1024]{2,1,0:T(8,128)(2,1)} async-done(((bf16[4,128,1024]{2,1,0:T(8,128)(2,1)}), bf16[1,128,1024]{2,1,0:T(8,128)(2,1)}) %reduce-scatter.13.cloned.1.call-update) | async-done | bytes 262160 | tf_op jit(solution)/shard_map/reduce_scatter | solution.py:269
  376.4 15.5 %all-gather.20.cloned.1.call-done = bf16[4,128,1024]{2,1,0:T(8,128)(2,1)} async-done(((bf16[1,128,1024]{2,1,0:T(8,128)(2,1)}), bf16[4,128,1024]{2,1,0:T(8,128)(2,1)}) %all-gather.20.cloned.1.call-update) | async-done | bytes 1048592 | tf_op jit(solution)/shard_map/all_gather | solution.py:278
  404.9 4.6 collective-permute-start.2
  414.0 5.5 collective-permute-done.2
  434.6 4.0 fusion.72
  441.1 3.9 fusion.73
  445.1 5.0 reduce-scatter.15.cloned.1.call-done
  451.4 39.4 %all-reduce.5 = (f32[1024]{0:T(1024)S(1)}, f32[1024]{0:T(1024)S(1)}) all-reduce(f32[1024]{0:T(1024)S(1)} %get-tuple-element.58, f32[1024]{0:T(1024)S(1)} %copy-done.32), channel_id=6, replica_groups=mesh['seq'=8,'fsdp'=4] {'seq','fsdp'}, use_global_device_ids=true, to_apply=%region_20.21.clone | all-reduce | flops 2048 | bytes 16384
  494.3 60.6 %reduce-scatter.23.cloned.1.call-done = f32[128,656]{0,1:T(8,128)} async-done(((f32[1024,656]{0,1:T(8,128)}), f32[128,656]{0,1:T(8,128)}) %reduce-scatter.23.cloned.1.call-update) | async-done | bytes 335888 | tf_op jit(solution)/shard_map/reduce_scatter | solution.py:364
  555.0 67.8 %reduce-scatter.19.cloned.1.call-done = f32[256,128]{1,0:T(8,128)} async-done(((f32[256,1024]{1,0:T(8,128)}), f32[256,128]{1,0:T(8,128)}) %reduce-scatter.19.cloned.1.call-update) | async-done | bytes 131088 | tf_op jit(solution)/shard_map/reduce_scatter | solution.py:362
  622.8 77.7 %reduce-scatter.17.cloned.1.call-done = f32[128,3,256]{2,0,1:T(8,128)} async-done(((f32[1024,3,256]{2,0,1:T(8,128)}), f32[128,3,256]{2,0,1:T(8,128)}) %reduce-scatter.17.cloned.1.call-update) | async-done | bytes 393232 | tf_op jit(solution)/shard_map/reduce_scatter | solution.py:359
  700.5 108.5 %reduce-scatter.21.cloned.1.call-done = f32[128,2,656]{0,2,1:T(8,128)} async-done(((f32[1024,2,656]{0,2,1:T(8,128)}), f32[128,2,656]{0,2,1:T(8,128)}) %reduce-scatter.21.cloned.1.call-update) | async-done | bytes 671760 | tf_op jit(solution)/shard_map/reduce_scatter | solution.py:363
  (224 shorter events, 77.1 us)
Async XLA Ops:
  7.2 64.6 %all-gather.8.cloned.1.call-start = ((), (), s32[]{:S(2)}) async-start(), calls=%async_computation.8 | async-start | bytes 1310720 | tf_op jit(solution)/shard_map/all_gather | solution.py:198
  50.9 67.9 %copy-start.28 = (f32[1024]{0:T(1024)}, f32[1024]{0:T(1024)S(1)}, u32[]{:S(2)}) copy-start(f32[1024]{0:T(1024)S(1)} %convert_element_type.138) | copy-start | bytes 12292
  55.1 63.7 %all-gather.10.cloned.1.call-start = ((), (), s32[]{:S(2)}) async-start(), calls=%async_computation.9 | async-start | bytes 1769472 | tf_op jit(solution)/shard_map/all_gather | solution.py:189
  56.9 142.0 %reduce-scatter.9.cloned.1.call-start = ((), (), s32[]{:S(2)}) async-start(), calls=%async_computation.10 | async-start | bytes 1310720 | tf_op jit(solution)/shard_map/reduce_scatter | solution.py:220
  59.4 62.4 %copy-start.22 = (f32[128,32]{0,1:T(8,128)}, f32[128,32]{0,1:T(8,128)S(1)}, u32[]{:S(2)}) copy-start(f32[128,32]{0,1:T(8,128)S(1)} %get-tuple-element.106) | copy-start | bytes 49156
  122.1 48.3 %collective-permute-start.1 = (bf16[4,64,512]{1,2,0:T(8,128)(2,1)S(1)}, bf16[4,64,512]{1,2,0:T(8,128)(2,1)S(1)}, u32[]{:S(2)}, u32[]{:S(2)}) collective-permute-start(bf16[4,64,512]{1,2,0:T(8,128)(2,1)S(1)} %get-tuple-element.98), channel_id=1, source_target_pairs={{4,0},{8,4},{12,8},{16,12},{20,16},{24,20},{28,24},{5,1},{9,5},{13... | collective-permute-start | bytes 786440 | tf_op jit(solution)/shard_map/ppermute | solution.py:21
  123.4 47.0 %collective-permute-start = (bf16[4,64,512]{1,2,0:T(8,128)(2,1)S(1)}, bf16[4,64,512]{1,2,0:T(8,128)(2,1)S(1)}, u32[]{:S(2)}, u32[]{:S(2)}) collective-permute-start(bf16[4,64,512]{1,2,0:T(8,128)(2,1)S(1)} %get-tuple-element.97), channel_id=1, source_target_pairs={{0,4},{4,8},{8,12},{12,16},{16,20},{20,24},{24,28},{1,5},{5,9},{9,... | collective-permute-start | bytes 786440 | tf_op jit(solution)/shard_map/ppermute | solution.py:20
  175.7 82.4 %all-gather.14.cloned.1.call-start = ((), (), s32[]{:S(2)}) async-start(), calls=%async_computation.12 | async-start | bytes 3022848 | tf_op jit(solution)/shard_map/all_gather | solution.py:191
  176.2 98.7 %all-gather.12.cloned.1.call-start = ((), (), s32[]{:S(2)}) async-start(), calls=%async_computation.11 | async-start | bytes 1310720 | tf_op jit(solution)/shard_map/all_gather | solution.py:229
  176.3 103.9 %copy-start.24 = (f32[1024]{0:T(1024)}, f32[1024]{0:T(1024)S(1)}, u32[]{:S(2)}) copy-start(f32[1024]{0:T(1024)S(1)} %convert_element_type.150) | copy-start | bytes 12292
  200.1 80.1 %copy-start.33 = (f32[128]{0:T(128)}, f32[128]{0:T(128)S(1)}, u32[]{:S(2)}) copy-start(f32[128]{0:T(128)S(1)} %broadcast_multiply_fusion.4) | copy-start | bytes 1540
  201.2 79.0 %copy-start.35 = (f32[128]{0:T(128)}, f32[128]{0:T(128)S(1)}, u32[]{:S(2)}) copy-start(f32[128]{0:T(128)S(1)} %add_rsqrt_fusion) | copy-start | bytes 1540
  203.1 90.0 %all-gather.18.cloned.1.call-start = ((), (), s32[]{:S(2)}) async-start(), calls=%async_computation.15 | async-start | bytes 1310720 | tf_op jit(solution)/shard_map/all_gather | solution.py:230
  203.6 133.4 %all-gather.16.cloned.1.call-start = ((), (), s32[]{:S(2)}) async-start(), calls=%async_computation.13 | async-start | bytes 1511424 | tf_op jit(solution)/shard_map/all_gather | solution.py:192
  204.4 165.6 %reduce-scatter.13.cloned.1.call-start = ((), (), s32[]{:S(2)}) async-start(), calls=%async_computation.16 | async-start | bytes 1310720 | tf_op jit(solution)/shard_map/reduce_scatter | solution.py:269
  346.9 45.0 %all-gather.20.cloned.1.call-start = ((), (), s32[]{:S(2)}) async-start(), calls=%async_computation.17 | async-start | bytes 1310720 | tf_op jit(solution)/shard_map/all_gather | solution.py:278
  375.0 75.1 %reduce-scatter.15.cloned.1.call-start = ((), (), s32[]{:S(2)}) async-start(), calls=%async_computation.18 | async-start | bytes 1310720 | tf_op jit(solution)/shard_map/reduce_scatter | solution.py:350
  403.5 10.5 %collective-permute-start.3 = (bf16[4,64,512]{2,1,0:T(8,128)(2,1)S(1)}, bf16[4,64,512]{2,1,0:T(8,128)(2,1)S(1)}, u32[]{:S(2)}, u32[]{:S(2)}) collective-permute-start(bf16[4,64,512]{2,1,0:T(8,128)(2,1)S(1)} %get-tuple-element.84), channel_id=1, source_target_pairs={{4,0},{8,4},{12,8},{16,12},{20,16},{24,20},{28,24},{5,1},{9,5},{13... | collective-permute-start | bytes 786440 | tf_op jit(solution)/shard_map/ppermute | solution.py:21
  404.9 14.5 %collective-permute-start.2 = (bf16[4,64,512]{2,1,0:T(8,128)(2,1)S(1)}, bf16[4,64,512]{2,1,0:T(8,128)(2,1)S(1)}, u32[]{:S(2)}, u32[]{:S(2)}) collective-permute-start(bf16[4,64,512]{2,1,0:T(8,128)(2,1)S(1)} %get-tuple-element.83), channel_id=1, source_target_pairs={{0,4},{4,8},{8,12},{12,16},{16,20},{20,24},{24,28},{1,5},{5,9},{9,... | collective-permute-start | bytes 786440 | tf_op jit(solution)/shard_map/ppermute | solution.py:20
  425.1 66.9 %reduce-scatter.11.cloned.1.call-start = ((), (), s32[]{:S(2)}) async-start(), calls=%async_computation.14 | async-start | bytes 1310720 | tf_op jit(solution)/shard_map/reduce_scatter | solution.py:241
  428.6 126.4 %reduce-scatter.23.cloned.1.call-start = ((), (), s32[]{:S(2)}) async-start(), calls=%async_computation.22 | async-start | bytes 3022848 | tf_op jit(solution)/shard_map/reduce_scatter | solution.py:364
  431.1 191.7 %reduce-scatter.19.cloned.1.call-start = ((), (), s32[]{:S(2)}) async-start(), calls=%async_computation.20 | async-start | bytes 1179648 | tf_op jit(solution)/shard_map/reduce_scatter | solution.py:362
  433.8 266.7 %reduce-scatter.17.cloned.1.call-start = ((), (), s32[]{:S(2)}) async-start(), calls=%async_computation.19 | async-start | bytes 3538944 | tf_op jit(solution)/shard_map/reduce_scatter | solution.py:359
  438.6 370.3 %reduce-scatter.21.cloned.1.call-start = ((), (), s32[]{:S(2)}) async-start(), calls=%async_computation.21 | async-start | bytes 6045696 | tf_op jit(solution)/shard_map/reduce_scatter | solution.py:363
  (42 other events, 571.0 us)
Sparse Core Ops, SparseCore 0:
  55.2 16.4 all-gather.7
  74.4 44.3 all-gather.9
  175.8 23.1 reduce-scatter.8
  200.8 57.1 all-gather.13
  260.0 14.8 all-gather.11
  276.4 16.6 all-gather.17
  295.1 41.9 all-gather.15
  347.0 22.9 reduce-scatter.12
  375.2 16.6 all-gather.19
  425.2 24.8 reduce-scatter.14
  452.6 24.8 reduce-scatter.10
  481.4 73.5 reduce-scatter.22
  558.9 63.7 reduce-scatter.18
  626.8 73.6 reduce-scatter.16
  704.5 104.3 reduce-scatter.20
where the time goes:
time: 817 us; the launch traced here: 815 us
  waiting for transfers between devices  578 us (71%)
  blocking collectives  124 us (15%)
  matrix products  43.8 us (5%)
  other arithmetic  24.2 us (3%)
  local copies, waits for them, and re-layouts  18.3 us (2%)
  between operations  14.8 us (2%)
  starting transfers between devices  12.7 us (2%)
    reduce_scatter x1, waiting for transfers between devices, per_device(): lax.psum_scatter(grad_in.reshape(width, 2, share), 'seq', scatter_dimensi...  108 us
    unnamed x2, blocking collectives  81.4 us
    reduce_scatter x1, waiting for transfers between devices, per_device(): lax.psum_scatter(grad_qkv.reshape(width, 3, quarter), 'seq', scatter_dime...  77.7 us
    reduce_scatter x1, waiting for transfers between devices, per_device(): lax.psum_scatter(grad_out_weight, 'seq', scatter_dimension=1, tiled=True)  67.8 us
    reduce_scatter x1, waiting for transfers between devices, per_device(): lax.psum_scatter(grad_down, 'seq', scatter_dimension=0, tiled=True)  60.6 us
    all_gather x1, waiting for transfers between devices, per_device(): lax.all_gather(in_weight, 'seq', axis=0, tiled=True)  53.6 us
    all_gather x1, waiting for transfers between devices, per_device(): lax.all_gather(qkv_weight, 'seq', axis=0, tiled=True)  47.1 us
    all_gather x1, waiting for transfers between devices, per_device(): lax.all_gather(down_weight, 'seq', axis=0, tiled=True)  44 us
  transfers between devices with their start and end apart: 19, of which 16 were waited for; matrix products, arithmetic and copies ran while one was open for 5% of the time, Pallas kernels for 0%

commit v1 on v0

--- a/solution.py
+++ b/solution.py
@@ -1,6 +1,10 @@
+import functools
+
 import jax
 import jax.numpy as jnp
 from jax import lax
+from jax.experimental import pallas as pl
+from jax.experimental.pallas import tpu as pltpu
 from jax.sharding import PartitionSpec as P
 
 HEAD = 64
@@ -8,6 +12,408 @@
 
 
 EPSILON = 1e-05
+
+
+class Place:
+    def __init__(self, axis):
+        self.axis = axis
+        self.n = lax.axis_size(axis)
+        self.length = self.n // 2
+        me = lax.axis_index(axis)
+        self.me = me
+        self.at = me // 2
+        self.side = me % 2
+
+    def partner(self):
+        return {self.axis: self.at * 2 + (1 - self.side)}
+
+    def right(self):
+        return {self.axis: self.me + 2}
+
+    def left(self):
+        return {self.axis: self.me - 2}
+
+    def has_right(self):
+        return self.at < self.length - 1
+
+    def has_left(self):
+        return self.at > 0
+
+    def greet(self, barrier):
+        mesh = pl.DeviceIdType.MESH
+        pl.semaphore_signal(barrier, inc=1, device_id=self.partner(), device_id_type=mesh)
+
+        @pl.when(self.has_left())
+        def _():
+            pl.semaphore_signal(barrier, inc=1, device_id=self.left(), device_id_type=mesh)
+
+        @pl.when(self.has_right())
+        def _():
+            pl.semaphore_signal(barrier, inc=1, device_id=self.right(), device_id_type=mesh)
+
+    def peers(self):
+        one, none = jnp.int32(1), jnp.int32(0)
+        return 1 + jnp.where(self.has_left(), one, none) + jnp.where(self.has_right(), one, none)
+
+
+def remote(src, dst, send, recv, device):
+    return pltpu.make_async_remote_copy(
+        src_ref=src,
+        dst_ref=dst,
+        send_sem=send,
+        recv_sem=recv,
+        device_id=device,
+        device_id_type=pl.DeviceIdType.MESH,
+    )
+
+
+class Gather:
+    scratch = staticmethod(
+        lambda n: [
+            pltpu.SemaphoreType.DMA((3, n)),
+            pltpu.SemaphoreType.DMA((n,)),
+            pltpu.SemaphoreType.DMA,
+        ]
+    )
+
+    def __init__(self, place, src, dst, sems):
+        self.place, self.src, self.dst = place, src, dst
+        self.send, self.recv, self.local = sems
+
+    def copy(self, way, block, device, own=False):
+        src = self.src if own else self.dst.at[block]
+        return remote(src, self.dst.at[block], self.send.at[way, block], self.recv.at[block], device)
+
+    def onward(self, block, own, act):
+        place = self.place
+        act(self.copy(0, block, place.partner(), own))
+
+    def start(self):
+        place = self.place
+        pltpu.make_async_copy(self.src, self.dst.at[place.me], self.local).start()
+        self.ahead(place.me, True, lambda c: c.start())
+        self.behind(place.me, True, lambda c: c.start())
+        self.onward(place.me, True, lambda c: c.start())
+
+    def ahead(self, block, own, act):
+        place = self.place
+
+        @pl.when(place.has_right())
+        def _():
+            act(self.copy(1, block, place.right(), own))
+
+    def behind(self, block, own, act):
+        place = self.place
+
+        @pl.when(place.has_left())
+        def _():
+            act(self.copy(2, block, place.left(), own))
+
+    def step(self, d):
+        place = self.place
+
+        @pl.when(place.at - d >= 0)
+        def _():
+            block = place.me - 2 * d
+            self.copy(1, block, place.partner()).wait_recv()
+            self.ahead(block, False, lambda c: c.start())
+            self.onward(block, False, lambda c: c.start())
+
+        @pl.when(place.at + d < place.length)
+        def _():
+            block = place.me + 2 * d
+            self.copy(2, block, place.partner()).wait_recv()
+            self.behind(block, False, lambda c: c.start())
+            self.onward(block, False, lambda c: c.start())
+
+    def finish(self):
+        place = self.place
+        pltpu.make_async_copy(self.src, self.dst.at[place.me], self.local).wait()
+
+        def arrived(i, carry):
+            self.copy(0, 2 * i + 1 - place.side, place.partner()).wait_recv()
+            self.onward(2 * i + place.side, False, lambda c: c.wait_send())
+
+            @pl.when(i <= place.at)
+            def _():
+                self.ahead(2 * i + place.side, False, lambda c: c.wait_send())
+
+            @pl.when(i >= place.at)
+            def _():
+                self.behind(2 * i + place.side, False, lambda c: c.wait_send())
+
+            return carry
+
+        lax.fori_loop(0, place.length, arrived, 0)
+
+
+class Reduce:
+    @staticmethod
+    def scratch(n, block, dtype):
+        length = n // 2
+        return [
+            pltpu.VMEM((length,) + block, dtype),
+            pltpu.VMEM((length,) + block, dtype),
+            pltpu.VMEM((length + 1,) + block, dtype),
+            pltpu.SemaphoreType.DMA((2, length)),
+            pltpu.SemaphoreType.DMA((length,)),
+            pltpu.SemaphoreType.DMA((length + 1,)),
+        ]
+
+    def __init__(self, place, src, dst, scratch):
+        self.place, self.src, self.dst = place, src, dst
+        self.stage, self.paired, self.lined, self.send, self.pair_recv, self.line_recv = scratch
+
+    def across(self, i):
+        place = self.place
+        return remote(
+            self.src.at[2 * i + 1 - place.side],
+            self.paired.at[i],
+            self.send.at[0, i],
+            self.pair_recv.at[i],
+            place.partner(),
+        )
+
+    def along(self, i, slot, device):
+        return remote(
+            self.stage.at[i], self.lined.at[slot], self.send.at[1, i], self.line_recv.at[slot], device
+        )
+
+    def start(self):
+        place = self.place
+
+        def each(k, carry):
+            d = place.length - 1 - k
+
+            @pl.when(place.at + d < place.length)
+            def _():
+                self.across(place.at + d).start()
+
+            @pl.when(jnp.logical_and(d > 0, place.at - d >= 0))
+            def _():
+                self.across(place.at - d).start()
+
+            return carry
+
+        lax.fori_loop(0, place.length, each, 0)
+
+    def add(self, out, refs):
+        rows = out.shape[0]
+        tile = 16 if rows % 16 == 0 else 8
+
+        def each(i, carry):
+            at = pl.ds(pl.multiple_of(i * tile, tile), tile)
+            total = refs[0][at, :].astype(jnp.float32)
+            for ref in refs[1:]:
+                total = total + ref[at, :].astype(jnp.float32)
+            out[at, :] = total.astype(out.dtype)
+            return carry
+
+        lax.fori_loop(0, rows // tile, each, 0)
+
+    def own(self, i):
+        self.across(i).wait_recv()
+        return [self.src.at[2 * i + self.place.side], self.paired.at[i]]
+
+    def step(self, d):
+        place = self.place
+
+        @pl.when(place.at + d < place.length)
+        def _():
+            i = place.at + d
+            refs = self.own(i)
+
+            @pl.when(place.has_left())
+            def _():
+                self.along(i, i, place.partner()).wait_recv()
+                self.add(self.stage.at[i], refs + [self.lined.at[i]])
+
+            @pl.when(jnp.logical_not(place.has_left()))
+            def _():
+                self.add(self.stage.at[i], refs)
+
+            self.along(i, i, place.right()).start()
+
+        @pl.when(place.at - d >= 0)
+        def _():
+            i = place.at - d
+            refs = self.own(i)
+
+            @pl.when(place.has_right())
+            def _():
+                self.along(i, i, place.partner()).wait_recv()
+                self.add(self.stage.at[i], refs + [self.lined.at[i]])
+
+            @pl.when(jnp.logical_not(place.has_right()))
+            def _():
+                self.add(self.stage.at[i], refs)
+
+            slot = jnp.where(d == 1, place.length, i)
+            self.along(i, slot, place.left()).start()
+
+    def last(self):
+        place = self.place
+        i, extra = place.at, place.length
+        refs = self.own(i)
+
+        @pl.when(place.has_left())
+        def _():
+            self.along(i, i, place.partner()).wait_recv()
+
+        @pl.when(place.has_right())
+        def _():
+            self.along(i, extra, place.partner()).wait_recv()
+
+        both = jnp.logical_and(place.has_left(), place.has_right())
+
+        @pl.when(both)
+        def _():
+            self.add(self.dst, refs + [self.lined.at[i], self.lined.at[extra]])
+
+        @pl.when(jnp.logical_and(place.has_left(), jnp.logical_not(both)))
+        def _():
+            self.add(self.dst, refs + [self.lined.at[i]])
+
+        @pl.when(jnp.logical_and(place.has_right(), jnp.logical_not(both)))
+        def _():
+            self.add(self.dst, refs + [self.lined.at[extra]])
+
+    def finish(self):
+        place = self.place
+
+        def each(i, carry):
+            self.across(i).wait_send()
+
+            @pl.when(i != place.at)
+            def _():
+                self.along(i, i, place.partner()).wait_send()
+
+            return carry
+
+        lax.fori_loop(0, place.length, each, 0)
+
+
+def greet_all(places):
+    barrier = pltpu.get_barrier_semaphore()
+    for place in places:
+        place.greet(barrier)
+    pl.semaphore_wait(barrier, sum(place.peers() for place in places))
+
+
+def steps(jobs, down):
+    length = jobs[0].place.length
+
+    def each(k, carry):
+        d = length - 1 - k if down else k + 1
+        for job in jobs:
+            job.step(d)
+        return carry
+
+    lax.fori_loop(0, length - 1, each, 0)
+
+
+def take(items, count):
+    return items[:count], items[count:]
+
+
+def comm_kernel(plan, *refs):
+    seq, fsdp = Place("seq"), Place("fsdp")
+    places = {"seq": seq, "fsdp": fsdp}
+    ins, rest = take(list(refs), len(plan))
+    outs, scratch = take(rest, len(plan))
+    jobs = []
+    for (kind, axis), src, dst in zip(plan, ins, outs):
+        place = places[axis]
+        if kind == "gather":
+            own, scratch = take(scratch, 3)
+            jobs.append((kind, axis, Gather(place, src, dst, own), None))
+        elif kind == "reduce":
+            own, scratch = take(scratch, 6)
+            jobs.append((kind, axis, Reduce(place, src, dst, own), None))
+        elif kind == "sum":
+            own, scratch = take(scratch, 6)
+            mid, scratch = take(scratch, 1)
+            sems, scratch = take(scratch, 3)
+            jobs.append((kind, axis, Reduce(place, src, mid[0], own), Gather(place, mid[0], dst, sems)))
+        elif kind == "gather2":
+            own, scratch = take(scratch, 3)
+            mid, scratch = take(scratch, 1)
+            sems, scratch = take(scratch, 3)
+            jobs.append((kind, axis, Gather(seq, src, mid[0], own), Gather(fsdp, mid[0], dst, sems)))
+        elif kind == "reduce2":
+            own, scratch = take(scratch, 6)
+            mid, scratch = take(scratch, 1)
+            sems, scratch = take(scratch, 3)
+            jobs.append((kind, axis, Reduce(seq, src, mid[0], own), Gather(fsdp, mid[0], dst, sems)))
+    greet_all((seq, fsdp))
+    ga = [j for k, a, j, _ in jobs if a == "seq" and isinstance(j, Gather)]
+    gb = [j for k, a, j, _ in jobs if a == "fsdp" and isinstance(j, Gather)]
+    ra = [j for k, a, j, _ in jobs if a == "seq" and isinstance(j, Reduce)]
+    rb = [j for k, a, j, _ in jobs if a == "fsdp" and isinstance(j, Reduce)]
+    second = [j for k, a, _, j in jobs if k == "sum"]
+    late = [j for k, a, _, j in jobs if k in ("gather2", "reduce2")]
+    for job in rb + ra + gb + ga:
+        job.start()
+    if rb:
+        steps(rb, True)
+    if ga:
+        steps(ga, False)
+    if gb:
+        steps(gb, False)
+    for job in rb:
+        job.last()
+    for job in second:
+        job.start()
+    if ra:
+        steps(ra, True)
+    for job in ra:
+        job.last()
+    if second:
+        steps(second, False)
+    for job in ga:
+        job.finish()
+    for job in late:
+        job.start()
+    if late:
+        steps(late, False)
+    for job in gb + rb + ra + second + late:
+        job.finish()
+
+
+def communicate(number, jobs):
+    sizes = {axis: lax.axis_size(axis) for axis in ("seq", "fsdp")}
+    shapes, scratch = [], []
+    for kind, axis, array, dtype in jobs:
+        n = sizes[axis]
+        if kind == "gather":
+            shapes.append((n,) + array.shape)
+            scratch += Gather.scratch(n)
+        elif kind == "gather2":
+            shapes.append((sizes["fsdp"], n) + array.shape)
+            scratch += Gather.scratch(n)
+            scratch += [pltpu.VMEM((n,) + array.shape, array.dtype)] + Gather.scratch(sizes["fsdp"])
+        else:
+            block = array.shape[1:]
+            scratch += Reduce.scratch(n, block, array.dtype)
+            if kind == "reduce":
+                shapes.append(block)
+            elif kind == "sum":
+                shapes.append(array.shape)
+                scratch += [pltpu.VMEM(block, dtype)] + Gather.scratch(n)
+            else:
+                shapes.append((sizes["fsdp"],) + block)
+                scratch += [pltpu.VMEM(block, dtype)] + Gather.scratch(sizes["fsdp"])
+    vmem = pl.BlockSpec(memory_space=pltpu.VMEM)
+    return pl.pallas_call(
+        functools.partial(comm_kernel, tuple((kind, axis) for kind, axis, _, _ in jobs)),
+        out_shape=[jax.ShapeDtypeStruct(s, j[3]) for s, j in zip(shapes, jobs)],
+        in_specs=[vmem] * len(jobs),
+        out_specs=[vmem] * len(jobs),
+        scratch_shapes=scratch,
+        compiler_params=pltpu.CompilerParams(
+            collective_id=number, has_side_effects=True, vmem_limit_bytes=60 * 1024 * 1024
+        ),
+    )(*[array for _, _, array, _ in jobs])
 
 
 def with_halo(value, sides, width):
@@ -38,7 +444,7 @@
         - jnp.mean(weighted, axis=-1, keepdims=True)
         - scaled * jnp.mean(weighted * scaled, axis=-1, keepdims=True)
     )
-    return (back, jnp.sum(grad * scaled, axis=0))
+    return back
 
 
 def gelu_parts(inner):
@@ -167,41 +573,51 @@
 ):
     tokens = layer_input[0]
     grad_rows = out_grad[0]
-    rows = tokens.shape[0]
-    width = tokens.shape[1]
+    rows, width = tokens.shape
     streams = doc_lengths.shape[0]
     quarter = qkv_weight.shape[2]
     heads_here = quarter // HEAD
     share = down_weight.shape[1]
     reach = WIN
     block = min(rows, 512)
+    n_seq, n_fsdp = lax.axis_size("seq"), lax.axis_size("fsdp")
+    stream = lax.axis_index("fsdp")
+    part = width // n_seq
+    piece = attn_gain.shape[0]
+    b16, f32 = jnp.bfloat16, jnp.float32
     first = lax.axis_index("seq") * rows
     positions = first + jnp.arange(rows, dtype=jnp.int32)
     outer = first - reach + jnp.arange(rows + 2 * reach, dtype=jnp.int32)
     ids_query = jax.vmap(doc_ids, in_axes=(0, None))(doc_lengths, positions)
     ids_key = jax.vmap(doc_ids, in_axes=(0, None))(doc_lengths, outer)
     cosine, sine = rope_tables(positions, HEAD)
-    gain_one, gain_two = (
-        lax.all_gather(attn_gain, ("seq", "fsdp"), axis=0, tiled=True),
-        lax.all_gather(mlp_gain, ("seq", "fsdp"), axis=0, tiled=True),
-    )
-    qkv_full, out_rows, in_full, down_full = (
-        lax.all_gather(qkv_weight, "seq", axis=0, tiled=True),
-        lax.all_gather(out_weight, "seq", axis=1, tiled=True),
-        lax.all_gather(in_weight, "seq", axis=0, tiled=True),
-        lax.all_gather(down_weight, "seq", axis=0, tiled=True),
-    )
-    qkv_flat = qkv_full.reshape(width, 3 * quarter)
-    in_flat = in_full.reshape(width, 2 * share)
-    resid_in = tokens.astype(jnp.float32)
-    scaled_one, inverse_one, normed_one = norm_forward(resid_in, gain_one)
-    normed_group = lax.all_gather(normed_one[None], "fsdp", axis=0, tiled=True)
-    group_one = normed_group.reshape(streams * rows, width)
-    projected = jnp.dot(group_one, qkv_flat, preferred_element_type=jnp.float32)
+    gains = jnp.pad(jnp.stack([attn_gain, mlp_gain]), ((0, 14), (0, 128 - piece)))
+    gains_all, tokens_all, grad_all, qkv_all, out_all, in_all, down_all = communicate(
+        1,
+        [
+            ("gather2", "seq", gains, b16),
+            ("gather", "fsdp", tokens, b16),
+            ("gather", "fsdp", grad_rows, b16),
+            ("gather", "seq", qkv_weight.reshape(part, 3 * quarter), b16),
+            ("gather", "seq", out_weight, b16),
+            ("gather", "seq", in_weight.reshape(part, 2 * share), b16),
+            ("gather", "seq", down_weight, b16),
+        ],
+    )
+    gain_one = gains_all[:, :, 0, :piece].transpose(1, 0, 2).reshape(width)
+    gain_two = gains_all[:, :, 1, :piece].transpose(1, 0, 2).reshape(width)
+    qkv_flat = qkv_all.reshape(width, 3 * quarter)
+    in_flat = in_all.reshape(width, 2 * share)
+    down_full = down_all.reshape(width, share)
+    out_rows = out_all.transpose(1, 0, 2).reshape(quarter, width)
+    grad_flat = grad_all.reshape(streams * rows, width)
+    resid_in = tokens_all.reshape(streams * rows, width).astype(f32)
+    scaled_one, inverse_one, group_one = norm_forward(resid_in, gain_one)
+    projected = jnp.dot(group_one, qkv_flat, preferred_element_type=f32)
     split = projected.reshape(streams, rows, 3, heads_here, HEAD)
-    query = rotate(split[:, :, 0], cosine, sine).astype(jnp.bfloat16)
-    keys = rotate(split[:, :, 1], cosine, sine).astype(jnp.bfloat16)
-    values = split[:, :, 2].astype(jnp.bfloat16)
+    query = rotate(split[:, :, 0], cosine, sine).astype(b16)
+    keys = rotate(split[:, :, 1], cosine, sine).astype(b16)
+    values = split[:, :, 2].astype(b16)
     packed = jnp.concatenate(
         [keys.reshape(streams, rows, quarter), values.reshape(streams, rows, quarter)], axis=2
     )
@@ -216,74 +632,55 @@
 
     attended, log_total = jax.vmap(forward_stream)(query, ext_keys, ext_values, ids_query, ids_key)
     attended_flat = attended.reshape(streams * rows, quarter)
-    partial_attn = jnp.dot(attended_flat, out_rows, preferred_element_type=jnp.float32)
-    attn_sum = lax.psum_scatter(
-        partial_attn.reshape(streams, rows, width).astype(jnp.bfloat16),
-        "fsdp",
-        scatter_dimension=0,
-        tiled=True,
-    ).astype(jnp.float32)
-    middle = resid_in + attn_sum[0]
-    scaled_two, inverse_two, normed_two = norm_forward(middle, gain_two)
-    normed_all, grad_all = (
-        lax.all_gather(normed_two[None], "fsdp", axis=0, tiled=True),
-        lax.all_gather(grad_rows[None], "fsdp", axis=0, tiled=True),
-    )
-    normed_flat = normed_all.reshape(streams * rows, width)
-    grad_flat = grad_all.reshape(streams * rows, width)
-    hidden = jnp.dot(normed_flat, in_flat, preferred_element_type=jnp.float32)
+    partial_attn = jnp.dot(attended_flat, out_rows, preferred_element_type=f32)
+    (attn_sum,) = communicate(
+        2, [("sum", "fsdp", partial_attn.astype(b16).reshape(streams, rows, width), b16)]
+    )
+    middle = resid_in + attn_sum.reshape(streams * rows, width).astype(f32)
+    scaled_two, inverse_two, normed_flat = norm_forward(middle, gain_two)
+    hidden = jnp.dot(normed_flat, in_flat, preferred_element_type=f32)
     inner, gate = (hidden[:, :share], hidden[:, share:])
     activated, slope = gelu_parts(inner)
-    mixed = (activated * gate).astype(jnp.bfloat16)
+    mixed = (activated * gate).astype(b16)
     partial_down = lax.dot_general(
-        mixed, down_full, (((1,), (1,)), ((), ())), preferred_element_type=jnp.float32
-    )
-    projected_down = lax.psum_scatter(
-        partial_down.reshape(streams, rows, width).astype(jnp.bfloat16),
-        "fsdp",
-        scatter_dimension=0,
-        tiled=True,
-    ).astype(jnp.float32)
-    output = (middle + projected_down[0]).astype(jnp.bfloat16)
-    qkv_full, out_rows, in_full, down_full = (
-        lax.all_gather(qkv_weight, "seq", axis=0, tiled=True),
-        lax.all_gather(out_weight, "seq", axis=1, tiled=True),
-        lax.all_gather(in_weight, "seq", axis=0, tiled=True),
-        lax.all_gather(down_weight, "seq", axis=0, tiled=True),
-    )
-    qkv_flat = qkv_full.reshape(width, 3 * quarter)
-    in_flat = in_full.reshape(width, 2 * share)
+        mixed, down_full, (((1,), (1,)), ((), ())), preferred_element_type=f32
+    )
     grad_down = lax.dot_general(
-        grad_flat, mixed, (((0,), (0,)), ((), ())), preferred_element_type=jnp.float32
-    )
-    grad_mixed = jnp.dot(grad_flat, down_full, preferred_element_type=jnp.float32)
+        grad_flat, mixed, (((0,), (0,)), ((), ())), preferred_element_type=f32
+    )
+    grad_mixed = jnp.dot(grad_flat, down_full, preferred_element_type=f32)
     grad_hidden = jnp.concatenate(
         [grad_mixed * gate * slope, grad_mixed * activated], axis=1
-    ).astype(jnp.bfloat16)
+    ).astype(b16)
     grad_in = lax.dot_general(
-        normed_flat, grad_hidden, (((0,), (0,)), ((), ())), preferred_element_type=jnp.float32
+        normed_flat, grad_hidden, (((0,), (0,)), ((), ())), preferred_element_type=f32
     )
     partial_back = lax.dot_general(
-        grad_hidden, in_flat, (((1,), (1,)), ((), ())), preferred_element_type=jnp.float32
-    )
-    grad_normed_two = lax.psum_scatter(
-        partial_back.reshape(streams, rows, width).astype(jnp.bfloat16),
-        "fsdp",
-        scatter_dimension=0,
-        tiled=True,
-    ).astype(jnp.float32)[0]
-    back_two, grad_gain_two = norm_backward(grad_normed_two, scaled_two, inverse_two, gain_two)
-    grad_middle = grad_rows.astype(jnp.float32) + back_two
-    grad_middle_b = grad_middle.astype(jnp.bfloat16)
-    grad_group = lax.all_gather(grad_middle_b[None], "fsdp", axis=0, tiled=True).reshape(
-        streams * rows, width
-    )
+        grad_hidden, in_flat, (((1,), (1,)), ((), ())), preferred_element_type=f32
+    )
+    grad_gain_two = jnp.sum(partial_back * scaled_two, axis=0)
+    back_sum, down_sum, summed_in, summed_down = communicate(
+        3,
+        [
+            ("sum", "fsdp", partial_back.astype(b16).reshape(streams, rows, width), b16),
+            ("reduce", "fsdp", partial_down.astype(b16).reshape(streams, rows, width), f32),
+            ("reduce", "seq", grad_in.astype(b16).reshape(n_seq, part, 2 * share), f32),
+            ("reduce", "seq", grad_down.astype(b16).reshape(n_seq, part, share), f32),
+        ],
+    )
+    middle_own = lax.dynamic_slice_in_dim(middle, stream * rows, rows, axis=0)
+    output = (middle_own + down_sum).astype(b16)
+    back_two = norm_backward(
+        back_sum.reshape(streams * rows, width).astype(f32), scaled_two, inverse_two, gain_two
+    )
+    grad_middle = grad_flat.astype(f32) + back_two
+    grad_group = grad_middle.astype(b16)
     grad_out_weight = lax.dot_general(
-        attended_flat, grad_group, (((0,), (0,)), ((), ())), preferred_element_type=jnp.float32
+        grad_group, attended_flat, (((0,), (0,)), ((), ())), preferred_element_type=f32
     )
     grad_attended = lax.dot_general(
-        grad_group, out_rows, (((1,), (1,)), ((), ())), preferred_element_type=jnp.float32
-    ).astype(jnp.bfloat16)
+        grad_group, out_rows, (((1,), (1,)), ((), ())), preferred_element_type=f32
+    ).astype(b16)
 
     def backward_stream(
         stream_query,
@@ -342,39 +739,38 @@
         axis=1,
     ).astype(jnp.bfloat16)
     grad_qkv = lax.dot_general(
-        group_one, grad_projected, (((0,), (0,)), ((), ())), preferred_element_type=jnp.float32
+        group_one, grad_projected, (((0,), (0,)), ((), ())), preferred_element_type=f32
     )
     partial_one = lax.dot_general(
-        grad_projected, qkv_flat, (((1,), (1,)), ((), ())), preferred_element_type=jnp.float32
-    )
-    grad_normed_one = lax.psum_scatter(
-        partial_one.reshape(streams, rows, width).astype(jnp.bfloat16),
-        "fsdp",
-        scatter_dimension=0,
-        tiled=True,
-    ).astype(jnp.float32)[0]
-    back_one, grad_gain_one = norm_backward(grad_normed_one, scaled_one, inverse_one, gain_one)
-    input_grad = grad_middle + back_one
-    summed_qkv, summed_out, summed_in, summed_down = (
-        lax.psum_scatter(
-            grad_qkv.reshape(width, 3, quarter), "seq", scatter_dimension=0, tiled=True
-        ),
-        lax.psum_scatter(grad_out_weight, "seq", scatter_dimension=1, tiled=True),
-        lax.psum_scatter(grad_in.reshape(width, 2, share), "seq", scatter_dimension=0, tiled=True),
-        lax.psum_scatter(grad_down, "seq", scatter_dimension=0, tiled=True),
-    )
-    summed_gain_one, summed_gain_two = (
-        lax.psum_scatter(grad_gain_one, ("seq", "fsdp"), scatter_dimension=0, tiled=True),
-        lax.psum_scatter(grad_gain_two, ("seq", "fsdp"), scatter_dimension=0, tiled=True),
-    )
+        grad_projected, qkv_flat, (((1,), (1,)), ((), ())), preferred_element_type=f32
+    )
+    grad_gain_one = jnp.sum(partial_one * scaled_one, axis=0)
+    gain_parts = jnp.stack([grad_gain_one, grad_gain_two]).reshape(2, n_seq, part)
+    gain_parts = jnp.pad(gain_parts.transpose(1, 0, 2), ((0, 0), (0, 6), (0, -part % 128)))
+    gain_sums, one_sum, summed_qkv, summed_out = communicate(
+        4,
+        [
+            ("reduce2", "seq", gain_parts, f32),
+            ("reduce", "fsdp", partial_one.astype(b16).reshape(streams, rows, width), f32),
+            ("reduce", "seq", grad_qkv.astype(b16).reshape(n_seq, part, 3 * quarter), f32),
+            ("reduce", "seq", grad_out_weight.astype(b16).reshape(n_seq, part, quarter), f32),
+        ],
+    )
+    gain_sum = lax.dynamic_slice_in_dim(jnp.sum(gain_sums, axis=0), stream * piece, piece, axis=1)
+
+    def own_rows(array):
+        return lax.dynamic_slice_in_dim(array, stream * rows, rows, axis=0)
+
+    back_one = norm_backward(one_sum, own_rows(scaled_one), own_rows(inverse_one), gain_one)
+    input_grad = own_rows(grad_middle) + back_one
     return (
         output[None],
         input_grad[None],
-        summed_gain_one,
-        summed_qkv,
-        summed_out,
-        summed_gain_two,
-        summed_in,
+        gain_sum[0],
+        summed_qkv.reshape(part, 3, quarter),
+        summed_out.T,
+        gain_sum[1],
+        summed_in.reshape(part, 2, share),
         summed_down,
     )
 

time: 817 us -> 372 us (0.46)
  waiting for transfers between devices: 578 us -> 26.9 us
  Pallas kernels: 0 us -> 229 us
  blocking collectives: 124 us -> 0 us
  local copies, waits for them, and re-layouts: 18.3 us -> 39.1 us
  between operations: 14.8 us -> 1.48 us
    reduce_scatter x8 -> x0, waiting for transfers between devices: 365 us -> none  [the longest x1 108 us: per_device(): lax.psum_scatter(grad_in.reshape(width, 2, share), 'seq', scatter_dimensi...]
    pallas_call x0 -> x4, Pallas kernels: none -> 229 us  [communicate(): pl.pallas_call(functools.partial(comm_kernel, tuple(((kind, axis) for kin...]
    all_gather x7 -> x0, waiting for transfers between devices: 202 us -> none  [the longest x1 53.6 us: per_device(): lax.all_gather(in_weight, 'seq', axis=0, tiled=True)]
    unnamed x2 -> x0, blocking collectives: 81.4 us -> none
    all_gather x1 -> x0, blocking collectives: 42.3 us -> none  [per_device(): lax.all_gather(out_weight, 'seq', axis=1, tiled=True)]
    ppermute x2, waiting for transfers between devices: 5.5 us -> 20.2 us  [with_halo(): before = lax.ppermute(last, axis, up)]
  transfers between devices with their start and end apart: 19 -> 4, of which waited for: 16 -> 3; matrix products, arithmetic and copies ran while one was open for 5% -> 2% of each run, Pallas kernels for 0% -> 0%
where the time goes in v1:
time: 372 us; the launch traced here: 370 us
  Pallas kernels  229 us (62%)
  local copies, waits for them, and re-layouts  39.1 us (11%)
  matrix products  35.9 us (10%)
  other arithmetic  28.8 us (8%)
  waiting for transfers between devices  26.9 us (7%)
  starting transfers between devices  8.69 us (2%)
    pallas_call x4, Pallas kernels, communicate(): pl.pallas_call(functools.partial(comm_kernel, tuple(((kind, axis) for kin...  229 us
    ppermute x2, waiting for transfers between devices, with_halo(): before = lax.ppermute(last, axis, up)  20.2 us
    unnamed x111, local copies, waits for them, and re-layouts  11.8 us
  transfers between devices with their start and end apart: 4, of which 3 were waited for; matrix products, arithmetic and copies ran while one was open for 2% of the time, Pallas kernels for 0%

profile of v1, /device:TPU:0, one launch (start us, length us, event | category | flops | bytes accessed | tf_op | source)
XLA Modules:
  0.0 370.3 jit_solution(3618346777579817627)
XLA Ops:
  2.6 1.7 copy.58.refs_6_
  4.3 1.9 copy.57.refs_5_
  7.5 86.8 %shard_map.152 = (bf16[4,8,16,128]{3,2,1,0:T(8,128)(2,1)}, bf16[4,128,1024]{2,1,0:T(8,128)(2,1)}, bf16[4,128,1024]{2,1,0:T(8,128)(2,1)}, bf16[8,128,768]{2,1,0:T...) custom-call(bf16[16,128]{1,0:T(8,128)(2,1)} %fusion.50.refs_0_, ...), custom_call_target="tpu_custom_call" | custom-call | tf_op jit(solution)/shard_map/pallas_call | solution.py:407
  101.3 2.6 fusion.19
  105.6 2.5 collective-permute-start
  112.3 19.0 %collective-permute-done = bf16[4,64,512]{1,2,0:T(8,128)(2,1)S(1)} collective-permute-done((bf16[4,64,512]{1,2,0:T(8,128)(2,1)}, bf16[4,64,512]{1,2,0:T(8,128)(2,1)S(1)}, u32[]{:S(2)}, u32[]{:S(2)}) %collective-permute-start) | collective-permute-done | bytes 262176 | tf_op jit(solution)/shard_map/ppermute | solution.py:426
  137.9 25.0 %shard_map.153 = bf16[4,128,1024]{2,1,0:T(8,128)(2,1)} custom-call(bf16[4,128,1024]{2,1,0:T(8,128)(2,1)} %bitcast.162), custom_call_target="tpu_custom_call" | custom-call | tf_op jit(solution)/shard_map/pallas_call | solution.py:407
  168.6 2.5 fusion.14
  171.2 2.0 convolution_convert_fusion.3
  173.2 2.0 convolution_convert_fusion.2
  175.8 2.6 copy.68
  178.4 6.7 %multiply_reduce_fusion = (f32[1024]{0:T(1024)}, f32[512,1024]{1,0:T(8,128)S(1)}, f32[512,1024]{1,0:T(8,128)}, bf16[512,1024]{1,0:T(8,128)(2,1)}) fusion(f32[512]{0:T(512)S(1)} %get-tuple-element.170, f32[512]{0:T(512)S(1)} %get-tuple-element.168, bf16[4,128,1024]{2,1,0:T(8,128)(2,1)S(1)} %copy-done.1, bf16[4,128,1024]{2,1,0:T(8,128)(2,1)S(1)} %copy-done, ...), kind=kOutput, calls=%fused_computation.17 | convolution fusion | flops 1382611968 | bytes 11378688 | tf_op jit(solution)/shard_map/dot_general | solution.py:658
  186.3 3.1 convolution_convert_fusion
  189.5 4.5 %copy.67 = bf16[1024,1312]{1,0:T(8,128)(2,1)} copy(bf16[1024,1312]{0,1:T(8,128)(2,1)} %convolution_convert_fusion) | data formatting | bytes 5373952 | tf_op jit(solution)/shard_map/convert_element_type | solution.py:667
  194.0 71.3 %shard_map.154 = (bf16[4,128,1024]{2,1,0:T(8,128)(2,1)}, f32[128,1024]{1,0:T(8,128)}, f32[128,1312]{1,0:T(8,128)}, f32[128,656]{1,0:T(8,128)}) custom-call(bf16[4,128,1024]{2,1,0:T(8,128)(2,1)} %bitcast.184, bf16[4,128,1024]{2,1,0:T(8,128)(2,1)} %bitcast.182, bf16[8,128,1312]{2,1,0:T(8,128)(2,1)} %bitcast.158, bf16[8,128,656]{2,1,0:T(8,128)(2,1)} %bitcast.159), custom_call_target="tpu_custom_call" | custom-call | tf_op jit(solution)/shard_map/pallas_call | solution.py:407
  265.3 2.2 multiply_reduce_fusion.4
  287.3 2.2 copy.80
  289.6 3.6 collective-permute-start.2
  294.6 1.8 fusion.39
  298.9 6.7 %collective-permute-done.3 = bf16[4,64,512]{2,1,0:T(8,128)(2,1)S(1)} collective-permute-done((bf16[4,64,512]{2,1,0:T(8,128)(2,1)S(1)}, bf16[4,64,512]{2,1,0:T(8,128)(2,1)S(1)}, u32[]{:S(2)}, u32[]{:S(2)}) %collective-permute-start.3) | collective-permute-done | bytes 262176 | tf_op jit(solution)/shard_map/ppermute | solution.py:427
  308.9 3.3 fusion.65
  312.2 2.3 convolution_convert_fusion.1
  315.1 46.4 %shard_map.155 = (f32[4,8,128]{2,1,0:T(8,128)}, f32[128,1024]{1,0:T(8,128)}, f32[128,768]{1,0:T(8,128)}, f32[128,256]{1,0:T(8,128)}) custom-call(f32[8,8,128]{2,1,0:T(8,128)} %pad.19.refs_0_, bf16[4,128,1024]{2,1,0:T(8,128)(2,1)} %bitcast.183, bf16[8,128,768]{2,1,0:T(8,128)(2,1)} %bitcast.179, bf16[8,128,256]{2,1,0:T(8,128)(2,1)} %bitcast.195), custom_call_target="tpu_custom_call" | custom-call | tf_op jit(solution)/shard_map/pallas_call | solution.py:407
  367.9 2.4 fusion.35
  (204 shorter events, 64.0 us)
Async XLA Ops:
  94.3 5.5 %copy-start.16 = (bf16[8,128,768]{2,1,0:T(8,128)(2,1)S(1)}, bf16[8,128,768]{2,1,0:T(8,128)(2,1)}, u32[]{:S(2)}) copy-start(bf16[8,128,768]{2,1,0:T(8,128)(2,1)} %get-tuple-element.85) | copy-start | bytes 4718596
  95.4 6.0 %copy-start.36 = (f32[1024]{0:T(1024)}, f32[1024]{0:T(1024)S(1)}, u32[]{:S(2)}) copy-start(f32[1024]{0:T(1024)S(1)} %reshape.601) | copy-start | bytes 12292
  104.0 5.4 %copy-start.39 = (s32[4,5]{1,0:T(4,128)S(1)}, s32[4,5]{1,0:T(4,128)}, u32[]{:S(2)}) copy-start(s32[4,5]{1,0:T(4,128)} %param.10) | copy-start | bytes 244
  104.4 28.6 %copy-start.18 = (bf16[4,128,4,32]{1,3,2,0:T(8,128)(2,1)}, bf16[4,128,4,32]{1,3,2,0:T(8,128)(2,1)S(1)}, u32[]{:S(2)}) copy-start(bf16[4,128,4,32]{1,3,2,0:T(8,128)(2,1)S(1)} %get-tuple-element.147) | copy-start | bytes 393220
  105.6 25.7 %collective-permute-start = (bf16[4,64,512]{1,2,0:T(8,128)(2,1)}, bf16[4,64,512]{1,2,0:T(8,128)(2,1)S(1)}, u32[]{:S(2)}, u32[]{:S(2)}) collective-permute-start(bf16[4,64,512]{1,2,0:T(8,128)(2,1)} %get-tuple-element.150), channel_id=1, source_target_pairs={{0,4},{4,8},{8,12},{12,16},{16,20},{20,24},{24,28},{1,5},{5,9},{9,... | collective-permute-start | bytes 786440 | tf_op jit(solution)/shard_map/ppermute | solution.py:426
  108.0 23.2 %collective-permute-start.1 = (bf16[4,64,512]{1,2,0:T(8,128)(2,1)}, bf16[4,64,512]{1,2,0:T(8,128)(2,1)}, u32[]{:S(2)}, u32[]{:S(2)}) collective-permute-start(bf16[4,64,512]{1,2,0:T(8,128)(2,1)} %get-tuple-element.151), channel_id=1, source_target_pairs={{4,0},{8,4},{12,8},{16,12},{20,16},{24,20},{28,24},{5,1},{9,5},{13... | collective-permute-start | bytes 786440 | tf_op jit(solution)/shard_map/ppermute | solution.py:427
  110.9 157.7 %copy-start.33 = (f32[1024]{0:T(1024)}, f32[1024]{0:T(1024)S(1)}, u32[]{:S(2)}) copy-start(f32[1024]{0:T(1024)S(1)} %reshape.603) | copy-start | bytes 12292
  112.1 24.3 %copy-start.9 = (bf16[256,8,128]{0,2,1:T(8,128)(2,1)}, bf16[256,8,128]{0,2,1:T(8,128)(2,1)S(1)}, u32[]{:S(2)}) copy-start(bf16[256,8,128]{0,2,1:T(8,128)(2,1)S(1)} %copy.65) | copy-start | bytes 1572868
  178.4 8.0 %copy-start.50 = (bf16[512,656]{0,1:T(8,128)(2,1)S(1)}, bf16[512,656]{0,1:T(8,128)(2,1)}, u32[]{:S(2)}) copy-start(bf16[512,656]{0,1:T(8,128)(2,1)} %get-tuple-element.128) | copy-start | bytes 2015236
  178.4 8.0 %copy-start.51 = (bf16[512,656]{0,1:T(8,128)(2,1)S(1)}, bf16[512,656]{0,1:T(8,128)(2,1)}, u32[]{:S(2)}) copy-start(bf16[512,656]{0,1:T(8,128)(2,1)} %get-tuple-element.129) | copy-start | bytes 2015236
  269.6 5.5 %copy-start.3 = (f32[4,4,128,256]{3,2,1,0:T(8,128)S(1)}, f32[4,4,128,256]{3,2,1,0:T(8,128)}, u32[]{:S(2)}) copy-start(f32[4,4,128,256]{3,2,1,0:T(8,128)} %copy-done.2) | copy-start | bytes 6291460
  289.5 5.1 %copy-start.25 = (f32[128,1024]{1,0:T(8,128)S(1)}, f32[128,1024]{1,0:T(8,128)}, u32[]{:S(2)}) copy-start(f32[128,1024]{1,0:T(8,128)} %get-tuple-element.90) | copy-start | bytes 1572868
  289.5 7.0 %copy-start.21 = (bf16[4,128,4,64]{1,0,3,2:T(4,128)(2,1)S(1)}, bf16[4,128,4,64]{1,0,3,2:T(4,128)(2,1)}, u32[]{:S(2)}) copy-start(bf16[4,128,4,64]{1,0,3,2:T(4,128)(2,1)} %copy-done.20) | copy-start | bytes 786436
  289.5 7.0 %copy-start.24 = (bf16[4,128,1024]{2,1,0:T(8,128)(2,1)S(1)}, bf16[4,128,1024]{2,1,0:T(8,128)(2,1)}, u32[]{:S(2)}) copy-start(bf16[4,128,1024]{2,1,0:T(8,128)(2,1)} %copy-done.23) | copy-start | bytes 3145732
  289.6 9.3 %collective-permute-start.2 = (bf16[4,64,512]{2,1,0:T(8,128)(2,1)S(1)}, bf16[4,64,512]{2,1,0:T(8,128)(2,1)S(1)}, u32[]{:S(2)}, u32[]{:S(2)}) collective-permute-start(bf16[4,64,512]{2,1,0:T(8,128)(2,1)S(1)} %get-tuple-element.138), channel_id=1, source_target_pairs={{0,4},{4,8},{8,12},{12,16},{16,20},{20,24},{24,28},{1,5},{5,9},{9,... | collective-permute-start | bytes 786440 | tf_op jit(solution)/shard_map/ppermute | solution.py:426
  293.3 12.3 %collective-permute-start.3 = (bf16[4,64,512]{2,1,0:T(8,128)(2,1)S(1)}, bf16[4,64,512]{2,1,0:T(8,128)(2,1)S(1)}, u32[]{:S(2)}, u32[]{:S(2)}) collective-permute-start(bf16[4,64,512]{2,1,0:T(8,128)(2,1)S(1)} %get-tuple-element.139), channel_id=1, source_target_pairs={{4,0},{8,4},{12,8},{16,12},{20,16},{24,20},{28,24},{5,1},{9,5},{13... | collective-permute-start | bytes 786440 | tf_op jit(solution)/shard_map/ppermute | solution.py:427
  297.7 8.3 %copy-start.43 = (pred[128]{0:T(512)(128)(4,1)S(1)}, pred[128]{0:T(512)(128)(4,1)}, u32[]{:S(2)}) copy-start(pred[128]{0:T(512)(128)(4,1)} %constant.106.clone.1) | copy-start | bytes 388
  314.5 48.5 %copy-start.27 = (f32[512,1024]{1,0:T(8,128)S(1)}, f32[512,1024]{1,0:T(8,128)}, u32[]{:S(2)}) copy-start(f32[512,1024]{1,0:T(8,128)} %copy-done.26) | copy-start | bytes 6291460
  361.5 6.4 %copy-start.11 = (f32[128,1024]{1,0:T(8,128)S(1)}, f32[128,1024]{1,0:T(8,128)}, u32[]{:S(2)}) copy-start(f32[128,1024]{1,0:T(8,128)} %get-tuple-element.92) | copy-start | bytes 1572868
  361.5 6.4 %copy-start.34 = (f32[1024]{0:T(1024)S(1)}, f32[1024]{0:T(1024)}, u32[]{:S(2)}) copy-start(f32[1024]{0:T(1024)} %copy-done.33) | copy-start | bytes 12292
  361.6 6.4 %copy-start.44 = (f32[128]{0:T(128)S(1)}, f32[128]{0:T(128)}, u32[]{:S(2)}) copy-start(f32[128]{0:T(128)} %fusion.51) | copy-start | bytes 1540
  361.6 6.4 %copy-start.45 = (f32[128]{0:T(128)S(1)}, f32[128]{0:T(128)}, u32[]{:S(2)}) copy-start(f32[128]{0:T(128)} %dynamic-slice.2) | copy-start | bytes 1540
  361.6 6.4 %copy-start.46 = (f32[128]{0:T(128)S(1)}, f32[128]{0:T(128)}, u32[]{:S(2)}) copy-start(f32[128]{0:T(128)} %dynamic-slice) | copy-start | bytes 1540
  361.6 6.4 %copy-start.47 = (f32[128]{0:T(128)S(1)}, f32[128]{0:T(128)}, u32[]{:S(2)}) copy-start(f32[128]{0:T(128)} %dynamic-slice.1) | copy-start | bytes 1540
  (32 other events, 66.6 us)

commit v2 on v1

--- a/solution.py
+++ b/solution.py
@@ -50,6 +50,10 @@
         @pl.when(self.has_right())
         def _():
             pl.semaphore_signal(barrier, inc=1, device_id=self.right(), device_id_type=mesh)
+
+    def diagonal(self):
+        there = jnp.where(self.side == 1, self.has_right(), self.has_left())
+        return there, {self.axis: self.me + 2 * self.side - 1}
 
     def peers(self):
         one, none = jnp.int32(1), jnp.int32(0)
@@ -293,15 +297,84 @@
         lax.fori_loop(0, place.length, each, 0)
 
 
-def greet_all(places):
+class Halo:
+    scratch = staticmethod(lambda: [pltpu.SemaphoreType.DMA((2,)), pltpu.SemaphoreType.DMA((2,))])
+
+    def __init__(self, place, src, mid, sems):
+        self.place, self.src, self.mid = place, src, mid
+        self.send, self.recv = sems
+        self.after = place.me < place.n - 1
+        self.before = place.me > 0
+
+    def copy(self, way):
+        rows, width = self.src.shape[0], self.mid.shape[1]
+        at = rows - width if way == 0 else 0
+        other = {self.place.axis: self.place.me + 1 - 2 * way}
+        return remote(
+            self.src.at[pl.ds(at, width)],
+            self.mid.at[way],
+            self.send.at[way],
+            self.recv.at[way],
+            other,
+        )
+
+    def start(self):
+        @pl.when(self.after)
+        def _():
+            self.copy(0).start()
+
+        @pl.when(self.before)
+        def _():
+            self.copy(1).start()
+
+        @pl.when(jnp.logical_not(self.before))
+        def _():
+            self.mid[0] = jnp.zeros(self.mid.shape[1:], self.mid.dtype)
+
+        @pl.when(jnp.logical_not(self.after))
+        def _():
+            self.mid[1] = jnp.zeros(self.mid.shape[1:], self.mid.dtype)
+
+    def arrive(self):
+        @pl.when(self.before)
+        def _():
+            self.copy(0).wait_recv()
+
+        @pl.when(self.after)
+        def _():
+            self.copy(1).wait_recv()
+
+    def finish(self):
+        @pl.when(self.after)
+        def _():
+            self.copy(0).wait_send()
+
+        @pl.when(self.before)
+        def _():
+            self.copy(1).wait_send()
+
+
+def greet_all(places, slanted):
     barrier = pltpu.get_barrier_semaphore()
+    extra = jnp.int32(0)
+    if slanted:
+        there, device = places[0].diagonal()
+        extra = jnp.where(there, jnp.int32(1), jnp.int32(0))
+
+        @pl.when(there)
+        def _():
+            pl.semaphore_signal(
+                barrier, inc=1, device_id=device, device_id_type=pl.DeviceIdType.MESH
+            )
+
     for place in places:
         place.greet(barrier)
-    pl.semaphore_wait(barrier, sum(place.peers() for place in places))
-
-
-def steps(jobs, down):
+    pl.semaphore_wait(barrier, extra + sum(place.peers() for place in places))
+
+
+def steps(jobs, down, skip=0, stop=None):
     length = jobs[0].place.length
+    stop = length - 1 if stop is None else min(stop, length - 1)
 
     def each(k, carry):
         d = length - 1 - k if down else k + 1
@@ -309,7 +382,8 @@
             job.step(d)
         return carry
 
-    lax.fori_loop(0, length - 1, each, 0)
+    if skip < stop:
+        lax.fori_loop(skip, stop, each, 0)
 
 
 def take(items, count):
@@ -323,7 +397,7 @@
     outs, scratch = take(rest, len(plan))
     jobs = []
     for (kind, axis), src, dst in zip(plan, ins, outs):
-        place = places[axis]
+        place = places.get(axis)
         if kind == "gather":
             own, scratch = take(scratch, 3)
             jobs.append((kind, axis, Gather(place, src, dst, own), None))
@@ -345,27 +419,40 @@
             mid, scratch = take(scratch, 1)
             sems, scratch = take(scratch, 3)
             jobs.append((kind, axis, Reduce(seq, src, mid[0], own), Gather(fsdp, mid[0], dst, sems)))
-    greet_all((seq, fsdp))
+        elif kind == "halo":
+            sems, scratch = take(scratch, 2)
+            mid, scratch = take(scratch, 1)
+            own, scratch = take(scratch, 3)
+            jobs.append((kind, axis, Halo(seq, src, mid[0], sems), Gather(fsdp, mid[0], dst, own)))
     ga = [j for k, a, j, _ in jobs if a == "seq" and isinstance(j, Gather)]
     gb = [j for k, a, j, _ in jobs if a == "fsdp" and isinstance(j, Gather)]
     ra = [j for k, a, j, _ in jobs if a == "seq" and isinstance(j, Reduce)]
     rb = [j for k, a, j, _ in jobs if a == "fsdp" and isinstance(j, Reduce)]
+    halos = [j for k, a, j, _ in jobs if k == "halo"]
+    rims = [j for k, a, _, j in jobs if k == "halo"]
     second = [j for k, a, _, j in jobs if k == "sum"]
     late = [j for k, a, _, j in jobs if k in ("gather2", "reduce2")]
-    for job in rb + ra + gb + ga:
+    greet_all((seq, fsdp), bool(halos))
+    for job in halos + rb + ra + gb + ga:
+        job.start()
+    for job in halos:
+        job.arrive()
+    for job in rims:
         job.start()
     if rb:
         steps(rb, True)
-    if ga:
-        steps(ga, False)
-    if gb:
-        steps(gb, False)
+    if ra:
+        steps(ra, True, stop=1)
     for job in rb:
         job.last()
     for job in second:
         job.start()
+    if ga:
+        steps(ga, False)
+    if gb:
+        steps(gb + rims, False)
     if ra:
-        steps(ra, True)
+        steps(ra, True, skip=1)
     for job in ra:
         job.last()
     if second:
@@ -376,7 +463,7 @@
         job.start()
     if late:
         steps(late, False)
-    for job in gb + rb + ra + second + late:
+    for job in halos + rims + gb + rb + ra + second + late:
         job.finish()
 
 
@@ -384,10 +471,15 @@
     sizes = {axis: lax.axis_size(axis) for axis in ("seq", "fsdp")}
     shapes, scratch = [], []
     for kind, axis, array, dtype in jobs:
-        n = sizes[axis]
+        n = sizes.get(axis)
         if kind == "gather":
             shapes.append((n,) + array.shape)
             scratch += Gather.scratch(n)
+        elif kind == "halo":
+            mid = (2, WIN, array.shape[1])
+            shapes.append((sizes["fsdp"],) + mid)
+            scratch += Halo.scratch() + [pltpu.VMEM(mid, array.dtype)]
+            scratch += Gather.scratch(sizes["fsdp"])
         elif kind == "gather2":
             shapes.append((sizes["fsdp"], n) + array.shape)
             scratch += Gather.scratch(n)
@@ -592,38 +684,37 @@
     ids_key = jax.vmap(doc_ids, in_axes=(0, None))(doc_lengths, outer)
     cosine, sine = rope_tables(positions, HEAD)
     gains = jnp.pad(jnp.stack([attn_gain, mlp_gain]), ((0, 14), (0, 128 - piece)))
-    gains_all, tokens_all, grad_all, qkv_all, out_all, in_all, down_all = communicate(
+    gains_all, rim_all, tokens_all, grad_all, qkv_all, out_all = communicate(
         1,
         [
             ("gather2", "seq", gains, b16),
+            ("halo", "both", tokens, b16),
             ("gather", "fsdp", tokens, b16),
             ("gather", "fsdp", grad_rows, b16),
             ("gather", "seq", qkv_weight.reshape(part, 3 * quarter), b16),
             ("gather", "seq", out_weight, b16),
-            ("gather", "seq", in_weight.reshape(part, 2 * share), b16),
-            ("gather", "seq", down_weight, b16),
         ],
     )
     gain_one = gains_all[:, :, 0, :piece].transpose(1, 0, 2).reshape(width)
     gain_two = gains_all[:, :, 1, :piece].transpose(1, 0, 2).reshape(width)
     qkv_flat = qkv_all.reshape(width, 3 * quarter)
-    in_flat = in_all.reshape(width, 2 * share)
-    down_full = down_all.reshape(width, share)
     out_rows = out_all.transpose(1, 0, 2).reshape(quarter, width)
     grad_flat = grad_all.reshape(streams * rows, width)
     resid_in = tokens_all.reshape(streams * rows, width).astype(f32)
     scaled_one, inverse_one, group_one = norm_forward(resid_in, gain_one)
-    projected = jnp.dot(group_one, qkv_flat, preferred_element_type=f32)
-    split = projected.reshape(streams, rows, 3, heads_here, HEAD)
-    query = rotate(split[:, :, 0], cosine, sine).astype(b16)
-    keys = rotate(split[:, :, 1], cosine, sine).astype(b16)
-    values = split[:, :, 2].astype(b16)
-    packed = jnp.concatenate(
-        [keys.reshape(streams, rows, quarter), values.reshape(streams, rows, quarter)], axis=2
-    )
-    extended = with_halo(packed, (("seq", 1),), WIN)
-    ext_keys = extended[:, :, :quarter].reshape(streams, -1, heads_here, HEAD)
-    ext_values = extended[:, :, quarter:].reshape(streams, -1, heads_here, HEAD)
+    rim_rows = streams * 2 * reach
+    normed_rim = norm_forward(rim_all.reshape(rim_rows, width).astype(f32), gain_one)[2]
+    normed_rim = normed_rim.reshape(streams, 2, reach, width)
+    normed_outer = jnp.concatenate(
+        [normed_rim[:, 0], group_one.reshape(streams, rows, width), normed_rim[:, 1]], axis=1
+    ).reshape(streams * (rows + 2 * reach), width)
+    outer_cosine, outer_sine = rope_tables(outer, HEAD)
+    projected = jnp.dot(group_one, qkv_flat[:, :quarter], preferred_element_type=f32)
+    query = rotate(projected.reshape(streams, rows, heads_here, HEAD), cosine, sine).astype(b16)
+    projected = jnp.dot(normed_outer, qkv_flat[:, quarter:], preferred_element_type=f32)
+    split = projected.reshape(streams, rows + 2 * reach, 2, heads_here, HEAD)
+    ext_keys = rotate(split[:, :, 0], outer_cosine, outer_sine).astype(b16)
+    ext_values = split[:, :, 1].astype(b16)
 
     def forward_stream(stream_query, stream_keys, stream_values, stream_ids, stream_key_ids):
         return attention_forward(
@@ -633,9 +724,16 @@
     attended, log_total = jax.vmap(forward_stream)(query, ext_keys, ext_values, ids_query, ids_key)
     attended_flat = attended.reshape(streams * rows, quarter)
     partial_attn = jnp.dot(attended_flat, out_rows, preferred_element_type=f32)
-    (attn_sum,) = communicate(
-        2, [("sum", "fsdp", partial_attn.astype(b16).reshape(streams, rows, width), b16)]
-    )
+    attn_sum, in_all, down_all = communicate(
+        2,
+        [
+            ("sum", "fsdp", partial_attn.astype(b16).reshape(streams, rows, width), b16),
+            ("gather", "seq", in_weight.reshape(part, 2 * share), b16),
+            ("gather", "seq", down_weight, b16),
+        ],
+    )
+    in_flat = in_all.reshape(width, 2 * share)
+    down_full = down_all.reshape(width, share)
     middle = resid_in + attn_sum.reshape(streams * rows, width).astype(f32)
     scaled_two, inverse_two, normed_flat = norm_forward(middle, gain_two)
     hidden = jnp.dot(normed_flat, in_flat, preferred_element_type=f32)

time: 372 us -> 340 us (0.914)
  waiting for transfers between devices: 26.9 us -> 0.01 us
  Pallas kernels: 229 us -> 216 us
  local copies, waits for them, and re-layouts: 39.1 us -> 45.7 us
  starting transfers between devices: 8.69 us -> 4.56 us
  matrix products: 35.9 us -> 39.9 us
    ppermute x2 -> x1, waiting for transfers between devices: 20.2 us -> 0.01 us  [with_halo(): before = lax.ppermute(last, axis, up)]
    pallas_call x4, Pallas kernels: 229 us -> 216 us  [communicate(): pl.pallas_call(functools.partial(comm_kernel, tuple(((kind, axis) for kin...]
    ppermute x2 -> x1, waiting for transfers between devices: 6.7 us -> 0.01 us  [with_halo(): after = lax.ppermute(first, axis, down)]
    dot_general x1 -> x4, local copies, waits for them, and re-layouts: 1.62 us -> 5.61 us  [the longest x2 2.98 us: per_device(): jnp.dot(group_one, qkv_flat[:, :quarter], preferred_element_type=f32)]
    unnamed x111 -> x131, local copies, waits for them, and re-layouts: 11.8 us -> 13.5 us
  transfers between devices with their start and end apart: 4 -> 2, of which waited for: 3 -> 0; matrix products, arithmetic and copies ran while one was open for 2% -> 5% of each run, Pallas kernels for 0% -> 0%
where the time goes in v2:
time: 340 us; the launch traced here: 339 us
  Pallas kernels  216 us (64%)
  local copies, waits for them, and re-layouts  45.7 us (13%)
  matrix products  39.9 us (12%)
  other arithmetic  30.8 us (9%)
  starting transfers between devices  4.56 us (1%)
    pallas_call x4, Pallas kernels, communicate(): pl.pallas_call(functools.partial(comm_kernel, tuple(((kind, axis) for kin...  216 us
    unnamed x131, local copies, waits for them, and re-layouts  13.5 us
  transfers between devices with their start and end apart: 2, of which 0 were waited for; matrix products, arithmetic and copies ran while one was open for 5% of the time, Pallas kernels for 0%

profile of v2, /device:TPU:0, one launch (start us, length us, event | category | flops | bytes accessed | tf_op | source)
XLA Modules:
  0.0 338.9 jit_solution(9020591948300181974)
XLA Ops:
  5.0 40.8 %shard_map.152 = (bf16[4,8,16,128]{3,2,1,0:T(8,128)(2,1)}, bf16[4,2,64,1024]{3,2,1,0:T(8,128)(2,1)}, bf16[4,128,1024]{2,1,0:T(8,128)(2,1)}, bf16[4,128,1024]{2,1...) custom-call(bf16[16,128]{1,0:T(8,128)(2,1)} %fusion.59.refs_0_, ...), custom_call_target="tpu_custom_call" | custom-call | tf_op jit(solution)/shard_map/pallas_call | solution.py:499
  45.8 2.0 slice_bitcast_fusion.2
  52.4 1.7 copy.68.refs_2_
  73.3 57.6 %shard_map.153 = (bf16[4,128,1024]{2,1,0:T(8,128)(2,1)}, bf16[8,128,1312]{2,1,0:T(8,128)(2,1)}, bf16[8,128,656]{2,1,0:T(8,128)(2,1)}) custom-call(bf16[4,128,1024]{2,1,0:T(8,128)(2,1)} %bitcast.167, bf16[128,1312]{1,0:T(8,128)(2,1)} %copy.67.refs_1_, bf16[128,656]{1,0:T(8,128)(2,1)} %copy.68.refs_2_), custom_call_target="tpu_custom_call" | custom-call | tf_op jit(solution)/shard_map/pallas_call | solution.py:499
  136.7 2.5 fusion.24
  139.2 2.0 convolution_convert_fusion.3
  141.3 2.0 convolution_convert_fusion.2
  143.3 2.5 copy.71
  145.8 6.7 %multiply_reduce_fusion = (f32[1024]{0:T(1024)}, f32[512,1024]{1,0:T(8,128)S(1)}, f32[512,1024]{1,0:T(8,128)}, bf16[512,1024]{1,0:T(8,128)(2,1)}) fusion(f32[512]{0:T(512)S(1)} %get-tuple-element.168, f32[512]{0:T(512)S(1)} %get-tuple-element.166, bf16[4,128,1024]{2,1,0:T(8,128)(2,1)S(1)} %copy-done.1, bf16[4,128,1024]{2,1,0:T(8,128)(2,1)S(1)} %copy-done, ...), kind=kOutput, calls=%fused_computation.30 | convolution fusion | flops 1382611968 | bytes 11378688 | tf_op jit(solution)/shard_map/dot_general | solution.py:756
  153.8 3.1 convolution_convert_fusion
  157.0 4.5 %copy.70 = bf16[1024,1312]{1,0:T(8,128)(2,1)} copy(bf16[1024,1312]{0,1:T(8,128)(2,1)} %convolution_convert_fusion) | data formatting | bytes 5373952 | tf_op jit(solution)/shard_map/convert_element_type | solution.py:765
  161.4 70.5 %shard_map.154 = (bf16[4,128,1024]{2,1,0:T(8,128)(2,1)}, f32[128,1024]{1,0:T(8,128)}, f32[128,1312]{1,0:T(8,128)}, f32[128,656]{1,0:T(8,128)}) custom-call(bf16[4,128,1024]{2,1,0:T(8,128)(2,1)} %bitcast.184, bf16[4,128,1024]{2,1,0:T(8,128)(2,1)} %bitcast.182, bf16[8,128,1312]{2,1,0:T(8,128)(2,1)} %bitcast.165, bf16[8,128,656]{2,1,0:T(8,128)(2,1)} %bitcast.166), custom_call_target="tpu_custom_call" | custom-call | tf_op jit(solution)/shard_map/pallas_call | solution.py:499
  232.0 2.2 multiply_reduce_fusion.4
  243.6 1.8 multiply_convert_fusion.1
  250.8 3.3 collective-permute-start
  255.4 2.6 convolution_convert_fusion.5
  262.6 1.9 copy.86
  264.4 2.2 copy.83
  266.6 2.0 fusion.46
  268.6 2.7 convolution_bitcast_fusion
  276.6 3.2 fusion.78
  279.9 2.2 convolution_convert_fusion.1
  282.7 47.5 %shard_map.155 = (f32[4,8,128]{2,1,0:T(8,128)}, f32[128,1024]{1,0:T(8,128)}, f32[128,768]{1,0:T(8,128)}, f32[128,256]{1,0:T(8,128)}) custom-call(f32[8,8,128]{2,1,0:T(8,128)} %pad.19.refs_0_, bf16[4,128,1024]{2,1,0:T(8,128)(2,1)} %bitcast.183, bf16[8,128,768]{2,1,0:T(8,128)(2,1)} %bitcast.177, bf16[8,128,256]{2,1,0:T(8,128)(2,1)} %bitcast.198), custom_call_target="tpu_custom_call" | custom-call | tf_op jit(solution)/shard_map/pallas_call | solution.py:499
  336.6 2.4 fusion.42
  (228 shorter events, 67.6 us)
Async XLA Ops:
  1.3 48.7 %copy-start.53 = (s32[128]{0:T(128)}, s32[128]{0:T(128)S(1)}, u32[]{:S(2)}) copy-start(s32[128]{0:T(128)S(1)} %get-tuple-element.179) | copy-start | bytes 1540
  1.8 48.8 %copy-start.43 = (s32[256]{0:T(256)}, s32[256]{0:T(256)S(1)}, u32[]{:S(2)}) copy-start(s32[256]{0:T(256)S(1)} %get-tuple-element.181) | copy-start | bytes 3076
  5.0 44.1 %copy-start.45 = (s32[4,5]{1,0:T(4,128)S(1)}, s32[4,5]{1,0:T(4,128)}, u32[]{:S(2)}) copy-start(s32[4,5]{1,0:T(4,128)} %param.10) | copy-start | bytes 244
  45.7 8.4 %copy-start.30 = (bf16[128,2,656]{0,2,1:T(8,128)(2,1)S(1)}, bf16[128,2,656]{0,2,1:T(8,128)(2,1)}, u32[]{:S(2)}) copy-start(bf16[128,2,656]{0,2,1:T(8,128)(2,1)} %param.15) | copy-start | bytes 1007620
  45.8 10.4 %copy-start = (bf16[4,128,1024]{2,1,0:T(8,128)(2,1)S(1)}, bf16[4,128,1024]{2,1,0:T(8,128)(2,1)}, u32[]{:S(2)}) copy-start(bf16[4,128,1024]{2,1,0:T(8,128)(2,1)} %get-tuple-element.85) | copy-start | bytes 3145732
  49.0 8.9 %copy-start.7 = (bf16[4,2,64,1024]{3,2,1,0:T(8,128)(2,1)S(1)}, bf16[4,2,64,1024]{3,2,1,0:T(8,128)(2,1)}, u32[]{:S(2)}) copy-start(bf16[4,2,64,1024]{3,2,1,0:T(8,128)(2,1)} %get-tuple-element.86) | copy-start | bytes 3145732
  56.1 179.2 %copy-start.39 = (f32[1024]{0:T(1024)}, f32[1024]{0:T(1024)S(1)}, u32[]{:S(2)}) copy-start(f32[1024]{0:T(1024)S(1)} %reshape.709) | copy-start | bytes 12292
  56.2 6.1 %copy-start.37 = (f32[1024]{0:T(1024)}, f32[1024]{0:T(1024)S(1)}, u32[]{:S(2)}) copy-start(f32[1024]{0:T(1024)S(1)} %reshape.707) | copy-start | bytes 12292
  58.0 4.2 %copy-start.47 = (f32[4,128]{1,0:T(4,128)}, f32[4,128]{1,0:T(4,128)S(1)}, u32[]{:S(2)}) copy-start(f32[4,128]{1,0:T(4,128)S(1)} %get-tuple-element.165) | copy-start | bytes 6148
  66.9 3.4 %copy-start.8 = (f32[4,256,2,4,64]{1,4,3,2,0:T(8,128)}, f32[4,256,2,4,64]{1,4,3,2,0:T(8,128)S(1)}, u32[]{:S(2)}) copy-start(f32[4,256,2,4,64]{1,4,3,2,0:T(8,128)S(1)} %fusion.6) | copy-start | bytes 6291460
  133.2 12.7 %copy-start.52 = (f32[512]{0:T(512)}, f32[512]{0:T(512)S(1)}, u32[]{:S(2)}) copy-start(f32[512]{0:T(512)S(1)} %get-tuple-element.168) | copy-start | bytes 6148
  145.8 8.0 %copy-start.60 = (bf16[512,656]{0,1:T(8,128)(2,1)S(1)}, bf16[512,656]{0,1:T(8,128)(2,1)}, u32[]{:S(2)}) copy-start(bf16[512,656]{0,1:T(8,128)(2,1)} %get-tuple-element.132) | copy-start | bytes 2015236
  145.8 8.0 %copy-start.61 = (bf16[512,656]{0,1:T(8,128)(2,1)S(1)}, bf16[512,656]{0,1:T(8,128)(2,1)}, u32[]{:S(2)}) copy-start(bf16[512,656]{0,1:T(8,128)(2,1)} %get-tuple-element.133) | copy-start | bytes 2015236
  232.0 3.3 copy-start.5
  236.4 5.7 %copy-start.3 = (f32[4,4,128,256]{3,2,1,0:T(8,128)S(1)}, f32[4,4,128,256]{3,2,1,0:T(8,128)}, u32[]{:S(2)}) copy-start(f32[4,4,128,256]{3,2,1,0:T(8,128)} %copy-done.2) | copy-start | bytes 6291460
  240.1 3.5 %copy-start.9 = (f32[4,256,2,4,64]{1,4,3,2,0:T(8,128)S(1)}, f32[4,256,2,4,64]{1,4,3,2,0:T(8,128)}, u32[]{:S(2)}) copy-start(f32[4,256,2,4,64]{1,4,3,2,0:T(8,128)} %copy-done.8) | copy-start | bytes 6291460
  250.8 20.5 %collective-permute-start = (bf16[4,64,512]{2,1,0:T(8,128)(2,1)S(1)}, bf16[4,64,512]{2,1,0:T(8,128)(2,1)}, u32[]{:S(2)}, u32[]{:S(2)}) collective-permute-start(bf16[4,64,512]{2,1,0:T(8,128)(2,1)S(1)} %get-tuple-element.142), channel_id=1, source_target_pairs={{0,4},{4,8},{8,12},{12,16},{16,20},{20,24},{24,28},{1,5},{5,9},{9,... | collective-permute-start | bytes 786440 | tf_op jit(solution)/shard_map/ppermute | solution.py:518
  254.1 17.2 %collective-permute-start.1 = (bf16[4,64,512]{2,1,0:T(8,128)(2,1)}, bf16[4,64,512]{2,1,0:T(8,128)(2,1)}, u32[]{:S(2)}, u32[]{:S(2)}) collective-permute-start(bf16[4,64,512]{2,1,0:T(8,128)(2,1)} %get-tuple-element.143), channel_id=1, source_target_pairs={{4,0},{8,4},{12,8},{16,12},{20,16},{24,20},{28,24},{5,1},{9,5},{13... | collective-permute-start | bytes 786440 | tf_op jit(solution)/shard_map/ppermute | solution.py:519
  255.4 2.6 copy-start.6
  276.6 3.2 copy-start.31
  276.6 3.2 copy-start.38
  282.1 49.6 %copy-start.26 = (f32[512,1024]{1,0:T(8,128)S(1)}, f32[512,1024]{1,0:T(8,128)}, u32[]{:S(2)}) copy-start(f32[512,1024]{1,0:T(8,128)} %copy-done.25) | copy-start | bytes 6291460
  330.2 6.3 %copy-start.12 = (f32[128,1024]{1,0:T(8,128)S(1)}, f32[128,1024]{1,0:T(8,128)}, u32[]{:S(2)}) copy-start(f32[128,1024]{1,0:T(8,128)} %get-tuple-element.96) | copy-start | bytes 1572868
  330.2 6.3 %copy-start.40 = (f32[1024]{0:T(1024)S(1)}, f32[1024]{0:T(1024)}, u32[]{:S(2)}) copy-start(f32[1024]{0:T(1024)} %copy-done.39) | copy-start | bytes 12292
  (40 other events, 57.2 us)

commit v3 on v2

--- a/solution.py
+++ b/solution.py
@@ -183,23 +183,16 @@
             self.stage.at[i], self.lined.at[slot], self.send.at[1, i], self.line_recv.at[slot], device
         )
 
-    def start(self):
-        place = self.place
-
-        def each(k, carry):
-            d = place.length - 1 - k
-
-            @pl.when(place.at + d < place.length)
-            def _():
-                self.across(place.at + d).start()
-
-            @pl.when(jnp.logical_and(d > 0, place.at - d >= 0))
-            def _():
-                self.across(place.at - d).start()
-
-            return carry
-
-        lax.fori_loop(0, place.length, each, 0)
+    def exchange(self, d):
+        place = self.place
+
+        @pl.when(place.at + d < place.length)
+        def _():
+            self.across(place.at + d).start()
+
+        @pl.when(jnp.logical_and(d > 0, place.at - d >= 0))
+        def _():
+            self.across(place.at - d).start()
 
     def add(self, out, refs):
         rows = out.shape[0]
@@ -384,6 +377,17 @@
 
     if skip < stop:
         lax.fori_loop(skip, stop, each, 0)
+
+
+def exchanges(jobs):
+    length = jobs[0].place.length
+
+    def each(k, carry):
+        for job in jobs:
+            job.exchange(length - 1 - k)
+        return carry
+
+    lax.fori_loop(0, length, each, 0)
 
 
 def take(items, count):
@@ -433,8 +437,11 @@
     second = [j for k, a, _, j in jobs if k == "sum"]
     late = [j for k, a, _, j in jobs if k in ("gather2", "reduce2")]
     greet_all((seq, fsdp), bool(halos))
-    for job in halos + rb + ra + gb + ga:
+    for job in halos + gb + ga:
         job.start()
+    for group in (rb, ra):
+        if group:
+            exchanges(group)
     for job in halos:
         job.arrive()
     for job in rims:
@@ -453,16 +460,24 @@
         steps(gb + rims, False)
     if ra:
         steps(ra, True, skip=1)
-    for job in ra:
-        job.last()
+    for group, act in ((ga, Gather.finish), (ra, Reduce.last)):
+        early = [j for k, _, j, _ in jobs if k in ("gather2", "reduce2") and j in group]
+        for job in early:
+            act(job)
+        if early:
+            for job in late:
+                job.start()
     if second:
         steps(second, False)
-    for job in ga:
-        job.finish()
-    for job in late:
-        job.start()
+    early = [j for k, _, j, _ in jobs if k in ("gather2", "reduce2")]
+    for job in ra:
+        if job not in early:
+            job.last()
     if late:
         steps(late, False)
+    for job in ga:
+        if job not in early:
+            job.finish()
     for job in halos + rims + gb + rb + ra + second + late:
         job.finish()
 
@@ -684,13 +699,12 @@
     ids_key = jax.vmap(doc_ids, in_axes=(0, None))(doc_lengths, outer)
     cosine, sine = rope_tables(positions, HEAD)
     gains = jnp.pad(jnp.stack([attn_gain, mlp_gain]), ((0, 14), (0, 128 - piece)))
-    gains_all, rim_all, tokens_all, grad_all, qkv_all, out_all = communicate(
+    gains_all, rim_all, tokens_all, qkv_all, out_all = communicate(
         1,
         [
             ("gather2", "seq", gains, b16),
             ("halo", "both", tokens, b16),
             ("gather", "fsdp", tokens, b16),
-            ("gather", "fsdp", grad_rows, b16),
             ("gather", "seq", qkv_weight.reshape(part, 3 * quarter), b16),
             ("gather", "seq", out_weight, b16),
         ],
@@ -699,7 +713,6 @@
     gain_two = gains_all[:, :, 1, :piece].transpose(1, 0, 2).reshape(width)
     qkv_flat = qkv_all.reshape(width, 3 * quarter)
     out_rows = out_all.transpose(1, 0, 2).reshape(quarter, width)
-    grad_flat = grad_all.reshape(streams * rows, width)
     resid_in = tokens_all.reshape(streams * rows, width).astype(f32)
     scaled_one, inverse_one, group_one = norm_forward(resid_in, gain_one)
     rim_rows = streams * 2 * reach
@@ -724,16 +737,18 @@
     attended, log_total = jax.vmap(forward_stream)(query, ext_keys, ext_values, ids_query, ids_key)
     attended_flat = attended.reshape(streams * rows, quarter)
     partial_attn = jnp.dot(attended_flat, out_rows, preferred_element_type=f32)
-    attn_sum, in_all, down_all = communicate(
+    attn_sum, grad_all, in_all, down_all = communicate(
         2,
         [
             ("sum", "fsdp", partial_attn.astype(b16).reshape(streams, rows, width), b16),
+            ("gather", "fsdp", grad_rows, b16),
             ("gather", "seq", in_weight.reshape(part, 2 * share), b16),
             ("gather", "seq", down_weight, b16),
         ],
     )
     in_flat = in_all.reshape(width, 2 * share)
     down_full = down_all.reshape(width, share)
+    grad_flat = grad_all.reshape(streams * rows, width)
     middle = resid_in + attn_sum.reshape(streams * rows, width).astype(f32)
     scaled_two, inverse_two, normed_flat = norm_forward(middle, gain_two)
     hidden = jnp.dot(normed_flat, in_flat, preferred_element_type=f32)

time: 340 us -> 307 us (0.903)
  Pallas kernels: 216 us -> 184 us
    pallas_call x4, Pallas kernels: 216 us -> 184 us  [communicate(): pl.pallas_call(functools.partial(comm_kernel, tuple(((kind, axis) for kin...]
where the time goes in v3:
time: 307 us; the launch traced here: 305 us
  Pallas kernels  184 us (60%)
  local copies, waits for them, and re-layouts  45.7 us (15%)
  matrix products  39.9 us (13%)
  other arithmetic  30.7 us (10%)
  starting transfers between devices  3.7 us (1%)
    pallas_call x4, Pallas kernels, communicate(): pl.pallas_call(functools.partial(comm_kernel, tuple(((kind, axis) for kin...  184 us
    unnamed x131, local copies, waits for them, and re-layouts  13.4 us
    dot_general x1, matrix products, per_device(): lax.dot_general(grad_hidden, in_flat, (((1,), (1,)), ((), ())), preferred...  6.61 us
  transfers between devices with their start and end apart: 2, of which 0 were waited for; matrix products, arithmetic and copies ran while one was open for 5% of the time, Pallas kernels for 0%

profile of v3, /device:TPU:0, one launch (start us, length us, event | category | flops | bytes accessed | tf_op | source)
XLA Modules:
  0.0 305.2 jit_solution(16505485364887800674)
XLA Ops:
  4.9 36.1 %shard_map.152 = (bf16[4,8,16,128]{3,2,1,0:T(8,128)(2,1)}, bf16[4,2,64,1024]{3,2,1,0:T(8,128)(2,1)}, bf16[4,128,1024]{2,1,0:T(8,128)(2,1)}, bf16[8,128,768]{2,1,0:T(8,128)(2,1)}, bf16[8,256,128]{2,1,0:T(8,128)(2,1)}) custom-call(bf16[16,128]{1,0:T(8,128)(2,1)} %fusion.59.refs_0_, bf16[128,1024]{1,0:T(8,128)(2,1)} %bitcast.186, bf16[128,1024]{1,0:T(8,128)(2,1)} %bitcast.187, ...), custom_call_target="tpu_custom_call" | custom-call | tf_op jit(solution)/shard_map/pallas_call | solution.py:514
  41.1 2.0 slice_bitcast_fusion.2
  47.7 1.7 copy.68.refs_3_
  68.5 57.8 %shard_map.153 = (bf16[4,128,1024]{2,1,0:T(8,128)(2,1)}, bf16[4,128,1024]{2,1,0:T(8,128)(2,1)}, bf16[8,128,1312]{2,1,0:T(8,128)(2,1)}, bf16[8,128,656]{2,1,0:T(8,128)(2,1)}) custom-call(bf16[4,128,1024]{2,1,0:T(8,128)(2,1)} %bitcast.167, bf16[128,1024]{1,0:T(8,128)(2,1)} %bitcast.201, bf16[128,1312]{1,0:T(8,128)(2,1)} %copy.67.refs_2_, ...), custom_call_target="tpu_custom_call" | custom-call | tf_op jit(solution)/shard_map/pallas_call | solution.py:514
  132.0 2.5 fusion.24
  134.6 2.0 convolution_convert_fusion.3
  136.6 2.0 convolution_convert_fusion.2
  138.6 2.5 copy.71
  141.2 6.6 %multiply_reduce_fusion = (f32[1024]{0:T(1024)}, f32[512,1024]{1,0:T(8,128)S(1)}, f32[512,1024]{1,0:T(8,128)}, bf16[512,1024]{1,0:T(8,128)(2,1)}) fusion(f32[512]{0:T(512)S(1)} %get-tuple-element.168, f32[512]{0:T(512)S(1)} %get-tuple-element.166, bf16[4,128,1024]{2,1,0:T(8,128)(2,1)S(1)} %copy-done.1, bf16[4,128,1024]{2,1,0:T(8,128)(2,1)S(1)} %copy-done, ...), kind=kOutput, calls=%fused_computation.30 | convolution fusion | flops 1382611968 | bytes 11378688 | tf_op jit(solution)/shard_map/dot_general | solution.py:771
  149.1 3.1 %convolution_convert_fusion = bf16[1024,1312]{0,1:T(8,128)(2,1)} fusion(f32[512,1024]{1,0:T(8,128)S(1)} %get-tuple-element.131, f32[1024]{0:T(1024)S(1)} %reshape.709, bf16[512,656]{0,1:T(8,128)(2,1)S(1)} %copy-done.61, bf16[512,656]{0,1:T(8,128)(2,1)S(1)} %copy-done.60), kind=kOutput, calls=%fused_computation | convolution fusion | flops 1380810752 | bytes 6131712 | tf_op jit(solution)/shard_map/dot_general | solution.py:768
  152.2 4.5 %copy.70 = bf16[1024,1312]{1,0:T(8,128)(2,1)} copy(bf16[1024,1312]{0,1:T(8,128)(2,1)} %convolution_convert_fusion) | data formatting | bytes 5373952 | tf_op jit(solution)/shard_map/convert_element_type | solution.py:780
  156.8 57.0 %shard_map.154 = (bf16[4,128,1024]{2,1,0:T(8,128)(2,1)}, f32[128,1024]{1,0:T(8,128)}, f32[128,1312]{1,0:T(8,128)}, f32[128,656]{1,0:T(8,128)}) custom-call(bf16[4,128,1024]{2,1,0:T(8,128)(2,1)} %bitcast.184, bf16[4,128,1024]{2,1,0:T(8,128)(2,1)} %bitcast.182, bf16[8,128,1312]{2,1,0:T(8,128)(2,1)} %bitcast.165, bf16[8,128,656]{2,1,0:T(8,128)(2,1)} %bitcast.166), custom_call_target="tpu_custom_call" | custom-call | tf_op jit(solution)/shard_map/pallas_call | solution.py:514
  213.8 2.2 multiply_reduce_fusion.4
  225.4 1.8 multiply_convert_fusion.1
  232.7 2.4 collective-permute-start
  236.4 2.7 convolution_convert_fusion.5
  243.7 1.9 copy.86
  245.6 2.2 copy.83
  247.7 2.0 fusion.46
  249.7 2.7 convolution_bitcast_fusion
  257.7 3.2 %fusion.78 = (bf16[512,1024]{1,0:T(8,128)(2,1)}, f32[1024]{0:T(1024)S(1)}, f32[512,1024]{1,0:T(8,128)S(1)}) fusion(f32[512]{0:T(512)S(1)} %copy-done.51, f32[512]{0:T(512)S(1)} %copy-done.50, bf16[4,128,1024]{2,1,0:T(8,128)(2,1)S(1)} %copy-done, bf16[1024,768]{1,0:T(8,128)(2,1)S(1)} %bitcast.181, bf16[512,256]{0,1:T(8,128)(2,1)} %copy.81, ...), kind=kOutput, calls=%fused_computation.183 | convolution fusion | flops 810810368 | bytes 6561792 | tf_op jit(solution)/shard_map/dot_general | solution.py:857
  261.0 2.2 convolution_convert_fusion.1
  263.8 32.7 %shard_map.155 = (f32[4,8,128]{2,1,0:T(8,128)}, f32[128,1024]{1,0:T(8,128)}, f32[128,768]{1,0:T(8,128)}, f32[128,256]{1,0:T(8,128)}) custom-call(f32[8,8,128]{2,1,0:T(8,128)} %pad.19.refs_0_, bf16[4,128,1024]{2,1,0:T(8,128)(2,1)} %bitcast.183, bf16[8,128,768]{2,1,0:T(8,128)(2,1)} %bitcast.177, bf16[8,128,256]{2,1,0:T(8,128)(2,1)} %bitcast.198), custom_call_target="tpu_custom_call" | custom-call | tf_op jit(solution)/shard_map/pallas_call | solution.py:514
  302.9 2.4 fusion.42
  (228 shorter events, 67.4 us)
Async XLA Ops:
  1.2 44.1 %copy-start.53 = (s32[128]{0:T(128)}, s32[128]{0:T(128)S(1)}, u32[]{:S(2)}) copy-start(s32[128]{0:T(128)S(1)} %get-tuple-element.179) | copy-start | bytes 1540
  1.7 44.2 %copy-start.43 = (s32[256]{0:T(256)}, s32[256]{0:T(256)S(1)}, u32[]{:S(2)}) copy-start(s32[256]{0:T(256)S(1)} %get-tuple-element.181) | copy-start | bytes 3076
  2.8 41.5 %copy-start.45 = (s32[4,5]{1,0:T(4,128)S(1)}, s32[4,5]{1,0:T(4,128)}, u32[]{:S(2)}) copy-start(s32[4,5]{1,0:T(4,128)} %param.10) | copy-start | bytes 244
  4.9 44.5 %copy-start.30 = (bf16[128,2,656]{0,2,1:T(8,128)(2,1)S(1)}, bf16[128,2,656]{0,2,1:T(8,128)(2,1)}, u32[]{:S(2)}) copy-start(bf16[128,2,656]{0,2,1:T(8,128)(2,1)} %param.15) | copy-start | bytes 1007620
  41.0 10.4 %copy-start = (bf16[4,128,1024]{2,1,0:T(8,128)(2,1)S(1)}, bf16[4,128,1024]{2,1,0:T(8,128)(2,1)}, u32[]{:S(2)}) copy-start(bf16[4,128,1024]{2,1,0:T(8,128)(2,1)} %get-tuple-element.85) | copy-start | bytes 3145732
  44.3 8.9 %copy-start.7 = (bf16[4,2,64,1024]{3,2,1,0:T(8,128)(2,1)S(1)}, bf16[4,2,64,1024]{3,2,1,0:T(8,128)(2,1)}, u32[]{:S(2)}) copy-start(bf16[4,2,64,1024]{3,2,1,0:T(8,128)(2,1)} %get-tuple-element.86) | copy-start | bytes 3145732
  51.3 165.8 %copy-start.39 = (f32[1024]{0:T(1024)}, f32[1024]{0:T(1024)S(1)}, u32[]{:S(2)}) copy-start(f32[1024]{0:T(1024)S(1)} %reshape.709) | copy-start | bytes 12292
  51.4 6.0 %copy-start.37 = (f32[1024]{0:T(1024)}, f32[1024]{0:T(1024)S(1)}, u32[]{:S(2)}) copy-start(f32[1024]{0:T(1024)S(1)} %reshape.707) | copy-start | bytes 12292
  53.2 4.2 %copy-start.47 = (f32[4,128]{1,0:T(4,128)}, f32[4,128]{1,0:T(4,128)S(1)}, u32[]{:S(2)}) copy-start(f32[4,128]{1,0:T(4,128)S(1)} %get-tuple-element.165) | copy-start | bytes 6148
  62.2 3.4 %copy-start.8 = (f32[4,256,2,4,64]{1,4,3,2,0:T(8,128)}, f32[4,256,2,4,64]{1,4,3,2,0:T(8,128)S(1)}, u32[]{:S(2)}) copy-start(f32[4,256,2,4,64]{1,4,3,2,0:T(8,128)S(1)} %fusion.6) | copy-start | bytes 6291460
  128.5 12.7 %copy-start.52 = (f32[512]{0:T(512)}, f32[512]{0:T(512)S(1)}, u32[]{:S(2)}) copy-start(f32[512]{0:T(512)S(1)} %get-tuple-element.168) | copy-start | bytes 6148
  141.2 8.0 %copy-start.60 = (bf16[512,656]{0,1:T(8,128)(2,1)S(1)}, bf16[512,656]{0,1:T(8,128)(2,1)}, u32[]{:S(2)}) copy-start(bf16[512,656]{0,1:T(8,128)(2,1)} %get-tuple-element.132) | copy-start | bytes 2015236
  141.2 8.0 %copy-start.61 = (bf16[512,656]{0,1:T(8,128)(2,1)S(1)}, bf16[512,656]{0,1:T(8,128)(2,1)}, u32[]{:S(2)}) copy-start(bf16[512,656]{0,1:T(8,128)(2,1)} %get-tuple-element.133) | copy-start | bytes 2015236
  213.8 3.3 %copy-start.5 = (bf16[4,128,1024]{2,1,0:T(8,128)(2,1)S(1)}, bf16[4,128,1024]{2,1,0:T(8,128)(2,1)}, u32[]{:S(2)}) copy-start(bf16[4,128,1024]{2,1,0:T(8,128)(2,1)} %get-tuple-element.95) | copy-start | bytes 3145732
  218.2 5.7 %copy-start.3 = (f32[4,4,128,256]{3,2,1,0:T(8,128)S(1)}, f32[4,4,128,256]{3,2,1,0:T(8,128)}, u32[]{:S(2)}) copy-start(f32[4,4,128,256]{3,2,1,0:T(8,128)} %copy-done.2) | copy-start | bytes 6291460
  221.9 3.5 %copy-start.9 = (f32[4,256,2,4,64]{1,4,3,2,0:T(8,128)S(1)}, f32[4,256,2,4,64]{1,4,3,2,0:T(8,128)}, u32[]{:S(2)}) copy-start(f32[4,256,2,4,64]{1,4,3,2,0:T(8,128)} %copy-done.8) | copy-start | bytes 6291460
  232.7 19.7 %collective-permute-start = (bf16[4,64,512]{2,1,0:T(8,128)(2,1)S(1)}, bf16[4,64,512]{2,1,0:T(8,128)(2,1)}, u32[]{:S(2)}, u32[]{:S(2)}) collective-permute-start(bf16[4,64,512]{2,1,0:T(8,128)(2,1)S(1)} %get-tuple-element.142), channel_id=1, source_target_pairs={{0,4},{4,8},{8,12},{12,16},{16,20},{20,24},{24,28},{1,5},{5,9},{9,... | collective-permute-start | bytes 786440 | tf_op jit(solution)/shard_map/ppermute | solution.py:533
  235.1 17.3 %collective-permute-start.1 = (bf16[4,64,512]{2,1,0:T(8,128)(2,1)}, bf16[4,64,512]{2,1,0:T(8,128)(2,1)}, u32[]{:S(2)}, u32[]{:S(2)}) collective-permute-start(bf16[4,64,512]{2,1,0:T(8,128)(2,1)} %get-tuple-element.143), channel_id=1, source_target_pairs={{4,0},{8,4},{12,8},{16,12},{20,16},{24,20},{28,24},{5,1},{9,5},{13... | collective-permute-start | bytes 786440 | tf_op jit(solution)/shard_map/ppermute | solution.py:534
  236.4 2.7 copy-start.6
  257.7 3.2 %copy-start.31 = (bf16[512,256]{0,1:T(8,128)(2,1)S(1)}, bf16[512,256]{0,1:T(8,128)(2,1)}, u32[]{:S(2)}) copy-start(bf16[512,256]{0,1:T(8,128)(2,1)} %copy.81) | copy-start | bytes 786436
  257.7 3.2 %copy-start.38 = (f32[1024]{0:T(1024)S(1)}, f32[1024]{0:T(1024)}, u32[]{:S(2)}) copy-start(f32[1024]{0:T(1024)} %copy-done.37) | copy-start | bytes 12292
  263.2 34.7 %copy-start.26 = (f32[512,1024]{1,0:T(8,128)S(1)}, f32[512,1024]{1,0:T(8,128)}, u32[]{:S(2)}) copy-start(f32[512,1024]{1,0:T(8,128)} %copy-done.25) | copy-start | bytes 6291460
  296.5 6.3 %copy-start.12 = (f32[128,1024]{1,0:T(8,128)S(1)}, f32[128,1024]{1,0:T(8,128)}, u32[]{:S(2)}) copy-start(f32[128,1024]{1,0:T(8,128)} %get-tuple-element.96) | copy-start | bytes 1572868
  296.5 6.3 %copy-start.40 = (f32[1024]{0:T(1024)S(1)}, f32[1024]{0:T(1024)}, u32[]{:S(2)}) copy-start(f32[1024]{0:T(1024)} %copy-done.39) | copy-start | bytes 12292
  (40 other events, 56.9 us)
